TPU v7x, 32 devices: a whole 2x2x4 slice. The times are simulated.
32 devices in a mesh: rep: 16 (over z, x, core), fsdp: 2 (over y).
Axes of the slice: x: 2, y: 2, z: 4, core: 2. Of those that a mesh axis runs over, the one named last changes fastest.
Arguments:
- tokens: bfloat16 [31520, 512], P(('rep', 'fsdp')), may hold values from -6 to 6
- cotangent: bfloat16 [31520, 512], P(('rep', 'fsdp')), may hold values from -6 to 6
- routes: int32 [31520, 2], P(('rep', 'fsdp')), may hold values from 0 to 31, all different within a row
- image_count: int32 [32], P(('rep', 'fsdp')), may hold values from 2 to 5, as said below
- capacity: int32 [32], P(('rep', 'fsdp')), may hold values from 40 to 80, as said below
- norm1_gain: bfloat16 [512], P('fsdp'), may hold values from 0.5 to 1.5
- norm1_bias: bfloat16 [512], P('fsdp'), may hold values from -1.25 to 1.25
- w_qkv: bfloat16 [512, 1536], P('fsdp'), may hold values from -0.25 to 0.25
- bias_q: bfloat16 [512], P('fsdp'), may hold values from -1.25 to 1.25
- bias_v: bfloat16 [512], P('fsdp'), may hold values from -1.25 to 1.25
- w_out: bfloat16 [512, 512], P('fsdp'), may hold values from -0.75 to 0.75
- bias_out: bfloat16 [512], P('fsdp'), may hold values from -0.625 to 0.625
- norm2_gain: bfloat16 [512], P('fsdp'), may hold values from 0.5 to 1.5
- norm2_bias: bfloat16 [512], P('fsdp'), may hold values from -1.25 to 1.25
- w_router: bfloat16 [512, 32], P('fsdp'), may hold values from -0.1875 to 0.1875
- expert_in: bfloat16 [32, 512, 2048], P('fsdp'), may hold values from -0.25 to 0.25
- expert_in_bias: bfloat16 [32, 2048], P('fsdp'), may hold values from -1.25 to 1.25
- expert_out: bfloat16 [32, 2048, 512], P('fsdp'), may hold values from -0.1875 to 0.1875
- expert_out_bias: bfloat16 [32, 512], P('fsdp'), may hold values from -0.625 to 0.625
Outputs:
- outputs: bfloat16 [31520, 512], P(('rep', 'fsdp'))
- grad_tokens: float32 [31520, 512], P(('rep', 'fsdp'))
- balance_loss: float32 [], replicated
- grad_norm1_gain: float32 [512], P('fsdp')
- grad_norm1_bias: float32 [512], P('fsdp')
- grad_w_qkv: float32 [512, 1536], P('fsdp')
- grad_bias_q: float32 [512], P('fsdp')
- grad_bias_v: float32 [512], P('fsdp')
- grad_w_out: float32 [512, 512], P('fsdp')
- grad_bias_out: float32 [512], P('fsdp')
- grad_norm2_gain: float32 [512], P('fsdp')
- grad_norm2_bias: float32 [512], P('fsdp')
- grad_w_router: float32 [512, 32], P('fsdp')
- grad_expert_in: float32 [32, 512, 2048], P('fsdp', None, 'rep')
- grad_expert_in_bias: float32 [32, 2048], P('fsdp', 'rep')
- grad_expert_out: float32 [32, 2048, 512], P('fsdp', 'rep')
- grad_expert_out_bias: float32 [32, 512], P('fsdp', 'rep')
Inputs may be any that keep to these rules, and one draw needn't show every extreme that they name: `image_count`: every device holds at least one image; some device holds 5. `capacity`: some device may fill 80 slots of each expert.
All inputs are finite; a program needn't handle non-finite values.
Results may differ from a plain program's by a relative error of at most 0.015.
Values may be sent and summed in bfloat16 or wider, within the bound.
A program may use at most 384 MiB of HBM per device.

v0:
```python
import jax
import jax.numpy as jnp
from jax import lax
from jax.experimental import pallas as pl
from jax.experimental.pallas import tpu as pltpu
from jax.sharding import PartitionSpec as P

HEADS = 8
HEAD_DIM = 64
EXPERTS = 32
IMG_TOK = 197
CAP = 80


def norm_rows(values, norm_gain, offset):
    average = jnp.mean(values, axis=-1, keepdims=True)
    centred = values - average
    variance = jnp.mean(centred * centred, axis=-1, keepdims=True)
    return centred * lax.rsqrt(variance + 1e-06) * norm_gain + offset


def slot_table(choices, alive_mask, limit, row_total):
    pair_expert = jnp.concatenate([choices[:, 0], choices[:, 1]])
    live_pairs = jnp.concatenate([alive_mask, alive_mask])
    expert_ids = jnp.arange(EXPERTS, dtype=jnp.int32)
    onehot = ((pair_expert[:, None] == expert_ids[None, :]) & live_pairs[:, None]).astype(jnp.int32)
    before = jnp.cumsum(onehot, axis=0) - onehot
    position = jnp.sum(before * onehot, axis=1)
    kept_pairs = live_pairs & (position < limit)
    pair_slot = pair_expert * CAP + position
    pair_token = jnp.concatenate(
        [jnp.arange(row_total, dtype=jnp.int32), jnp.arange(row_total, dtype=jnp.int32)]
    )
    slot_owner = jnp.full((EXPERTS * CAP,), row_total, jnp.int32)
    target = jnp.where(kept_pairs, pair_slot, EXPERTS * CAP)
    slot_owner = slot_owner.at[target].set(pair_token, mode="drop")
    safe_slot = jnp.where(kept_pairs, pair_slot, 0)
    return (slot_owner, kept_pairs, safe_slot, target, onehot)


def shards(
    tokens,
    cotangent,
    routes,
    image_count,
    capacity,
    norm1_gain,
    norm1_bias,
    w_qkv,
    bias_q,
    bias_v,
    w_out,
    bias_out,
    norm2_gain,
    norm2_bias,
    w_router,
    expert_in,
    expert_in_bias,
    expert_out,
    expert_out_bias,
):
    rows_count = tokens.shape[0]
    model_width = tokens.shape[1]
    image_total = rows_count // IMG_TOK
    score_scale = HEAD_DIM ** (-0.5)
    image_rows = jnp.arange(rows_count, dtype=jnp.int32) // IMG_TOK
    alive_mask = image_rows < image_count[0]
    alive_float = alive_mask.astype(jnp.float32)[:, None]
    slot_owner, kept_pairs, safe_slot, target, onehot = slot_table(
        routes, alive_mask, capacity[0], rows_count
    )
    kept_float = kept_pairs.astype(jnp.float32)
    load_local = jnp.sum(onehot.astype(jnp.float32), axis=0)
    live_local = jnp.sum(alive_float)
    load_total, live_total = lax.psum((load_local, live_local), ("rep", "fsdp"))
    gathered = (
        lax.all_gather(norm1_gain, "fsdp", axis=0, tiled=True),
        lax.all_gather(norm1_bias, "fsdp", axis=0, tiled=True),
        lax.all_gather(w_qkv, "fsdp", axis=0, tiled=True),
        lax.all_gather(bias_q, "fsdp", axis=0, tiled=True),
        lax.all_gather(bias_v, "fsdp", axis=0, tiled=True),
        lax.all_gather(w_out, "fsdp", axis=0, tiled=True),
        lax.all_gather(bias_out, "fsdp", axis=0, tiled=True),
        lax.all_gather(norm2_gain, "fsdp", axis=0, tiled=True),
        lax.all_gather(norm2_bias, "fsdp", axis=0, tiled=True),
        lax.all_gather(w_router, "fsdp", axis=0, tiled=True),
    )
    (
        gain_one,
        shift_one,
        qkv_full,
        query_bias,
        value_bias,
        out_full,
        out_bias,
        gain_two,
        shift_two,
        router_full,
    ) = gathered
    gain_one = gain_one.astype(jnp.float32)
    shift_one = shift_one.astype(jnp.float32)
    gain_two = gain_two.astype(jnp.float32)
    shift_two = shift_two.astype(jnp.float32)
    inputs = tokens.astype(jnp.float32)
    normed = norm_rows(inputs, gain_one, shift_one)
    normed_low = normed.astype(jnp.bfloat16)
    bias_row = jnp.concatenate([query_bias, jnp.zeros_like(query_bias), value_bias]).astype(
        jnp.float32
    )
    packed_low = (
        jnp.dot(normed_low, qkv_full, preferred_element_type=jnp.float32) + bias_row
    ).astype(jnp.bfloat16)
    image_shape = (image_total, IMG_TOK, HEADS, HEAD_DIM)
    queries = packed_low[:, :model_width].reshape(image_shape)
    all_keys = packed_low[:, model_width : 2 * model_width].reshape(image_shape)
    valued = packed_low[:, 2 * model_width :].reshape(image_shape)

    def score_block():
        return (
            jnp.einsum("iqhd,ikhd->hiqk", queries, all_keys, preferred_element_type=jnp.float32)
            * score_scale
        )

    scores = score_block()
    row_peak = jnp.max(scores, axis=-1, keepdims=True)
    exp_scores = jnp.exp(scores - row_peak)
    totals = jnp.sum(exp_scores, axis=-1, keepdims=True)
    log_total = row_peak + jnp.log(totals)
    attn_low = (exp_scores / totals).astype(jnp.bfloat16)
    mixed_low = (
        jnp.einsum("hiqk,ikhd->iqhd", attn_low, valued, preferred_element_type=jnp.float32)
        .reshape(rows_count, model_width)
        .astype(jnp.bfloat16)
    )
    middle = (
        inputs
        + jnp.dot(mixed_low, out_full, preferred_element_type=jnp.float32)
        + out_bias.astype(jnp.float32)
    )
    second_low = norm_rows(middle, gain_two, shift_two).astype(jnp.bfloat16)
    logits = jnp.dot(second_low, router_full, preferred_element_type=jnp.float32)
    expert_ids = jnp.arange(EXPERTS, dtype=jnp.int32)
    first_hot = (routes[:, 0:1] == expert_ids[None, :]).astype(jnp.float32)
    second_hot = (routes[:, 1:2] == expert_ids[None, :]).astype(jnp.float32)

    def gate_terms(logit_rows):
        router_probs = jax.nn.softmax(logit_rows, axis=-1)
        pick_one = jnp.sum(router_probs * first_hot, axis=-1)
        pick_two = jnp.sum(router_probs * second_hot, axis=-1)
        pick_total = pick_one + pick_two
        return (pick_one / pick_total, pick_two / pick_total, router_probs)

    (gate_first, gate_second, router_probs), gate_back = jax.vjp(gate_terms, logits)
    padded_rows = jnp.concatenate([second_low, jnp.zeros((1, model_width), jnp.bfloat16)], axis=0)
    sent_rows = padded_rows[slot_owner].reshape(EXPERTS, CAP, model_width)
    received = lax.all_to_all(sent_rows, "fsdp", split_axis=0, concat_axis=1, tiled=True)
    raised = (
        jnp.einsum("esd,edf->esf", received, expert_in, preferred_element_type=jnp.float32)
        + expert_in_bias.astype(jnp.float32)[:, None, :]
    )
    active, gelu_back = jax.vjp(jax.nn.gelu, raised)
    active_low = active.astype(jnp.bfloat16)
    produced = (
        jnp.einsum("esf,efd->esd", active_low, expert_out, preferred_element_type=jnp.float32)
        + expert_out_bias.astype(jnp.float32)[:, None, :]
    ).astype(jnp.bfloat16)
    returned = lax.all_to_all(produced, "fsdp", split_axis=1, concat_axis=0, tiled=True).reshape(
        EXPERTS * CAP, model_width
    )
    pair_rows = returned[safe_slot].astype(jnp.float32)
    pair_weight = jnp.concatenate([gate_first, gate_second]) * kept_float
    expert_sum = jnp.sum(
        (pair_rows * pair_weight[:, None]).reshape(2, rows_count, model_width), axis=0
    )
    outputs = (alive_float * (middle + expert_sum)).astype(jnp.bfloat16)
    upstream = cotangent.astype(jnp.float32) * alive_float
    pair_grad = jnp.concatenate([upstream, upstream], axis=0)
    gate_grads = jnp.sum(pair_grad * pair_rows, axis=1) * kept_float
    slot_gate = jnp.zeros((EXPERTS * CAP,), jnp.float32).at[target].set(pair_weight, mode="drop")
    padded_grad = jnp.concatenate([upstream, jnp.zeros((1, model_width), jnp.float32)], axis=0)
    slot_grads = (
        (padded_grad[slot_owner] * slot_gate[:, None])
        .astype(jnp.bfloat16)
        .reshape(EXPERTS, CAP, model_width)
    )
    grad_received = lax.all_to_all(slot_grads, "fsdp", split_axis=0, concat_axis=1, tiled=True)
    grad_active = jnp.einsum(
        "esd,efd->esf", grad_received, expert_out, preferred_element_type=jnp.float32
    )
    (grad_raised,) = gelu_back(grad_active)
    grad_raised_low = grad_raised.astype(jnp.bfloat16)
    grad_rows = jnp.einsum(
        "esf,edf->esd", grad_raised_low, expert_in, preferred_element_type=jnp.float32
    ).astype(jnp.bfloat16)
    back_rows = lax.all_to_all(grad_rows, "fsdp", split_axis=1, concat_axis=0, tiled=True).reshape(
        EXPERTS * CAP, model_width
    )
    expert_part = jnp.sum(
        (back_rows[safe_slot].astype(jnp.float32) * kept_float[:, None]).reshape(
            2, rows_count, model_width
        ),
        axis=0,
    )
    local_in = jnp.einsum(
        "esd,esf->edf", received, grad_raised_low, preferred_element_type=jnp.float32
    )
    local_in_bias = jnp.sum(grad_raised_low.astype(jnp.float32), axis=1)
    local_out = jnp.einsum(
        "esf,esd->efd", active_low, grad_received, preferred_element_type=jnp.float32
    )
    local_out_bias = jnp.sum(grad_received.astype(jnp.float32), axis=1)
    grad_in_weight, grad_in_bias, grad_out_weight, grad_out_expert_bias = (
        lax.psum_scatter(local_in, "rep", scatter_dimension=2, tiled=True),
        lax.psum_scatter(local_in_bias, "rep", scatter_dimension=1, tiled=True),
        lax.psum_scatter(local_out, "rep", scatter_dimension=1, tiled=True),
        lax.psum_scatter(local_out_bias, "rep", scatter_dimension=1, tiled=True),
    )
    prob_local = jnp.sum(router_probs * alive_float, axis=0)
    prob_total = lax.psum(prob_local, ("rep", "fsdp"))
    share = load_total / (2.0 * live_total)
    balance_loss = EXPERTS * jnp.sum(share * prob_total / live_total)
    aux_grad = alive_float * (EXPERTS * share / live_total)[None, :]
    (grad_logits,) = gate_back((gate_grads[:rows_count], gate_grads[rows_count:], aux_grad))
    grad_logits_low = grad_logits.astype(jnp.bfloat16)
    grad_router = jnp.dot(second_low.T, grad_logits_low, preferred_element_type=jnp.float32)
    grad_second = (
        jnp.dot(grad_logits_low, router_full.T, preferred_element_type=jnp.float32) + expert_part
    )
    _, norm_two_back = jax.vjp(norm_rows, middle, gain_two, shift_two)
    grad_mid_norm, grad_gain_two, grad_shift_two = norm_two_back(grad_second)
    grad_middle = upstream + grad_mid_norm
    grad_att_low = grad_middle.astype(jnp.bfloat16)
    grad_out_proj = jnp.dot(mixed_low.T, grad_att_low, preferred_element_type=jnp.float32)
    grad_out_bias = jnp.sum(grad_att_low.astype(jnp.float32), axis=0)
    grad_mixed = (
        jnp.dot(grad_att_low, out_full.T, preferred_element_type=jnp.float32)
        .astype(jnp.bfloat16)
        .reshape(image_shape)
    )
    recomputed = jnp.exp(score_block() - log_total)
    grad_weights = jnp.einsum(
        "iqhd,ikhd->hiqk", grad_mixed, valued, preferred_element_type=jnp.float32
    )
    grad_values = jnp.einsum(
        "hiqk,iqhd->ikhd",
        recomputed.astype(jnp.bfloat16),
        grad_mixed,
        preferred_element_type=jnp.float32,
    )
    inner_sum = jnp.sum(grad_weights * recomputed, axis=-1, keepdims=True)
    grad_scores = (recomputed * (grad_weights - inner_sum)).astype(jnp.bfloat16)
    grad_queries = (
        jnp.einsum("hiqk,ikhd->iqhd", grad_scores, all_keys, preferred_element_type=jnp.float32)
        * score_scale
    )
    grad_keys = (
        jnp.einsum("hiqk,iqhd->ikhd", grad_scores, queries, preferred_element_type=jnp.float32)
        * score_scale
    )
    grad_packed_low = jnp.concatenate(
        [
            grad_queries.reshape(rows_count, model_width),
            grad_keys.reshape(rows_count, model_width),
            grad_values.reshape(rows_count, model_width),
        ],
        axis=1,
    ).astype(jnp.bfloat16)
    grad_qkv = jnp.dot(normed_low.T, grad_packed_low, preferred_element_type=jnp.float32)
    packed_sums = jnp.sum(grad_packed_low.astype(jnp.float32), axis=0)
    grad_query_bias = packed_sums[:model_width]
    grad_value_bias = packed_sums[2 * model_width :]
    grad_normed = jnp.dot(grad_packed_low, qkv_full.T, preferred_element_type=jnp.float32)
    _, norm_one_back = jax.vjp(norm_rows, inputs, gain_one, shift_one)
    grad_input_norm, grad_gain_one, grad_shift_one = norm_one_back(grad_normed)
    grad_tokens = grad_middle + grad_input_norm
    local_grads = (
        grad_gain_one,
        grad_shift_one,
        grad_qkv,
        grad_query_bias,
        grad_value_bias,
        grad_out_proj,
        grad_out_bias,
        grad_gain_two,
        grad_shift_two,
        grad_router,
    )
    shares = (
        lax.psum_scatter(local_grads[0], "fsdp", scatter_dimension=0, tiled=True),
        lax.psum_scatter(local_grads[1], "fsdp", scatter_dimension=0, tiled=True),
        lax.psum_scatter(local_grads[2], "fsdp", scatter_dimension=0, tiled=True),
        lax.psum_scatter(local_grads[3], "fsdp", scatter_dimension=0, tiled=True),
        lax.psum_scatter(local_grads[4], "fsdp", scatter_dimension=0, tiled=True),
        lax.psum_scatter(local_grads[5], "fsdp", scatter_dimension=0, tiled=True),
        lax.psum_scatter(local_grads[6], "fsdp", scatter_dimension=0, tiled=True),
        lax.psum_scatter(local_grads[7], "fsdp", scatter_dimension=0, tiled=True),
        lax.psum_scatter(local_grads[8], "fsdp", scatter_dimension=0, tiled=True),
        lax.psum_scatter(local_grads[9], "fsdp", scatter_dimension=0, tiled=True),
    )
    owned = lax.psum(
        (
            shares[0],
            shares[1],
            shares[2],
            shares[3],
            shares[4],
            shares[5],
            shares[6],
            shares[7],
            shares[8],
            shares[9],
        ),
        "rep",
    )
    return (
        (outputs, grad_tokens, balance_loss)
        + tuple(owned)
        + (grad_in_weight, grad_in_bias, grad_out_weight, grad_out_expert_bias)
    )


def gelu_pair(value):
    root = 0.7978845608028654
    square = value * value
    bend = jnp.tanh(root * value * (1.0 + 0.044715 * square))
    half = 0.5 * (1.0 + bend)
    slope = half + 0.5 * value * (1.0 - bend * bend) * root * (1.0 + 3 * 0.044715 * square)
    return value * half, slope


def slice_grads_body(*refs, senders):
    parts, refs = refs[: sum(senders)], refs[sum(senders) :]
    in_ref, in_bias_ref, out_ref, keep_in, send_in, keep_out, send_out, d_bias, d_out_bias = refs
    core = lax.axis_index("rep") % 2
    width = in_ref.shape[1]

    def stacked(pieces):
        return jnp.concatenate([piece[...].reshape(-1, width) for piece in pieces], axis=0)

    rows = stacked(parts[: senders[0]])
    grads = stacked(parts[senders[0] :])
    first = in_ref[0]
    second = out_ref[0]
    raised = jnp.dot(rows, first, preferred_element_type=jnp.float32) + in_bias_ref[0].astype(
        jnp.float32
    )
    active, slope = gelu_pair(raised)
    active = active.astype(jnp.bfloat16)
    back = lax.dot_general(
        grads, second, (((1,), (1,)), ((), ())), preferred_element_type=jnp.float32
    )
    draised = (back * slope).astype(jnp.bfloat16)
    over_rows = (((0,), (0,)), ((), ()))
    g_in = lax.dot_general(rows, draised, over_rows, preferred_element_type=jnp.float32)
    g_out = lax.dot_general(active, grads, over_rows, preferred_element_type=jnp.float32)
    half = g_in.shape[1] // 2
    first_core = core == 0
    keep_in[0] = jnp.where(first_core, g_in[:, :half], g_in[:, half:])
    send_in[0] = jnp.where(first_core, g_in[:, half:], g_in[:, :half]).astype(jnp.bfloat16)
    keep_out[0] = jnp.where(first_core, g_out[:half], g_out[half:])
    send_out[0] = jnp.where(first_core, g_out[half:], g_out[:half]).astype(jnp.bfloat16)
    d_bias[0] = jnp.sum(draised.astype(jnp.float32), axis=0, keepdims=True)
    d_out_bias[0] = jnp.sum(grads.astype(jnp.float32), axis=0, keepdims=True)


def slice_grads(rows, grads, first, first_bias, second, chain, ident):
    experts, width, hidden = first.shape
    cap = rows[0].shape[2]
    slots = cap * sum(piece.shape[1] for piece in rows)
    part = 256
    half = part // 2
    f32 = jnp.float32
    def chip():
        return lax.axis_index("rep") // 2

    return run(
        lambda *refs: slice_grads_body(*refs, senders=(len(rows), len(grads))),
        (*rows, *grads, first, first_bias.reshape(experts, 1, hidden), second),
        [pl.BlockSpec((1,) + piece.shape[1:], lambda e: (e, 0, 0, 0)) for piece in (*rows, *grads)]
        + [
            pl.BlockSpec((1, width, part), lambda e: (e, 0, chip())),
            pl.BlockSpec((1, 1, part), lambda e: (e, 0, chip())),
            pl.BlockSpec((1, part, width), lambda e: (e, chip(), 0)),
        ],
        [by_image(width, half)] * 2 + [by_image(half, width)] * 2 + [by_image(1, part), by_image(1, width)],
        [
            jax.ShapeDtypeStruct((experts, width, half), f32),
            jax.ShapeDtypeStruct((experts, width, half), jnp.bfloat16),
            jax.ShapeDtypeStruct((experts, half, width), f32),
            jax.ShapeDtypeStruct((experts, half, width), jnp.bfloat16),
            jax.ShapeDtypeStruct((experts, 1, part), f32),
            jax.ShapeDtypeStruct((experts, 1, width), f32),
        ],
        grid=(experts,),
        cost=pl.CostEstimate(
            flops=8 * experts * slots * width * part,
            bytes_accessed=4 * experts * (slots * width + 3 * width * part),
            transcendentals=experts * slots * part,
        ),
        name="slice_grads",
        chain=chain,
        ident=ident,
    )


F32 = jnp.float32
BF16 = jnp.bfloat16
PAD = 208
ROOT_AXES = ("rep", "fsdp")
OVER_COLS = (((1,), (1,)), ((), ()))
OVER_ROWS = (((0,), (0,)), ((), ()))


def dot(left, right):
    return jnp.dot(left, right, preferred_element_type=F32)


def dot_cols(left, right):
    return lax.dot_general(left, right, OVER_COLS, preferred_element_type=F32)


def dot_rows(left, right):
    return lax.dot_general(left, right, OVER_ROWS, preferred_element_type=F32)


def iota(shape, axis):
    return lax.broadcasted_iota(jnp.int32, shape, axis)


def resident(shape):
    return pl.BlockSpec(shape, lambda *_: (0,) * len(shape))


def by_image(*shape):
    return pl.BlockSpec((1,) + shape, lambda i, *_: (i,) + (0,) * len(shape))


def scalar_spec():
    return pl.BlockSpec(memory_space=pltpu.SMEM)


def partner(link):
    device, side = lax.axis_index("rep"), lax.axis_index("fsdp")
    if link == "y":
        return {"rep": device, "fsdp": 1 - side}
    depth = device // 4
    step = {
        "core": 1 - 2 * (device % 2),
        "x": 2 - 4 * ((device // 2) % 2),
        "near": 4 - 8 * (depth % 2),
        "inner": 12 - 8 * depth,
        "skip": 8 - 16 * (depth // 2),
    }[link]
    return {"rep": device + step, "fsdp": side}


def only_if(condition, action):
    if condition is None:
        action()
    else:
        pl.when(condition)(action)


class Move:
    def __init__(self, link, source, target, needs=()):
        self.link, self.source, self.target, self.needs = link, source, target, needs

    def roles(self):
        depth = lax.axis_index("rep") // 4
        middle = (depth % 3) > 0
        if self.link == "inner":
            return middle, middle
        if self.link in ("outward", "skip"):
            return middle, (depth % 3) == 0
        return None, None

    def copy(self, refs, send, recv):
        return pltpu.make_async_remote_copy(
            src_ref=self.source(refs),
            dst_ref=self.target(refs),
            send_sem=send,
            recv_sem=recv,
            device_id=partner("near" if self.link == "outward" else self.link),
            device_id_type=pl.DeviceIdType.MESH,
        )


class Traffic:
    def __init__(self, sources, targets, rounds, steps):
        self.sources, self.targets, self.rounds, self.steps = sources, targets, rounds, steps

    def count(self):
        return sum(len(moves) for moves in self.rounds)

    def links(self):
        return {("near" if m.link == "outward" else m.link) for moves in self.rounds for m in moves}

    def start(self, which, refs, send, recv, arrived):
        moves = [m for moves in self.rounds for m in moves]
        at = sum(len(moves) for moves in self.rounds[:which])
        for k, move in enumerate(self.rounds[which]):
            for index in move.needs:
                if index not in arrived:
                    arrived.add(index)
                    only_if(moves[index].roles()[1], moves[index].copy(refs, send.at[index], recv.at[index]).wait_recv)
            only_if(move.roles()[0], move.copy(refs, send.at[at + k], recv.at[at + k]).start)

    def finish(self, refs, send, recv, arrived):
        moves = [m for moves in self.rounds for m in moves]
        for index, move in enumerate(moves):
            copy = move.copy(refs, send.at[index], recv.at[index])
            sends, receives = move.roles()
            only_if(sends, copy.wait_send)
            if index not in arrived:
                only_if(receives, copy.wait_recv)


def greet(links):
    barrier = pltpu.get_barrier_semaphore()
    middle = ((lax.axis_index("rep") // 4) % 3) > 0
    plain = [link for link in ("core", "x", "y", "near", "skip") if link in links]
    for link in plain:
        pl.semaphore_signal(barrier, inc=1, device_id=partner(link), device_id_type=pl.DeviceIdType.MESH)
    if "inner" in links:

        @pl.when(middle)
        def _():
            pl.semaphore_signal(
                barrier, inc=1, device_id=partner("inner"), device_id_type=pl.DeviceIdType.MESH
            )

    if "inner" in links:

        @pl.when(middle)
        def _():
            pl.semaphore_wait(barrier, len(plain) + 1)

        @pl.when(~middle)
        def _():
            if plain:
                pl.semaphore_wait(barrier, len(plain))

    else:
        pl.semaphore_wait(barrier, len(plain))


class Chain:
    def __init__(self, args, in_specs, out_specs, out_shape, scratch, links, actions):
        self.args, self.in_specs, self.out_specs, self.out_shape = args, in_specs, out_specs, out_shape
        self.scratch, self.links, self.actions = scratch, links, actions


def run(
    body, args, in_specs, out_specs, out_shape, *,
    name, grid=(1,), scratch=(), cost=None, traffic=None, chain=None, ident=None,
):
    if (traffic is None or traffic.count() == 0) and chain is None:
        outs = pl.pallas_call(
            body, grid=grid, in_specs=in_specs, out_specs=out_specs, out_shape=out_shape,
            scratch_shapes=list(scratch), cost_estimate=cost, name=name,
        )(*args)
        return outs, [], []
    traffic = traffic or Traffic([], [], [], [])
    chain = chain or Chain([], [], [], [], [], set(), [])
    n_in, n_src, n_out, n_dst = len(args), len(traffic.sources), len(out_shape), len(traffic.targets)
    anywhere = pl.BlockSpec(memory_space=pl.ANY)
    sizes = (n_in, n_src, len(chain.args), n_out, n_dst, len(chain.out_shape), len(scratch), len(chain.scratch))
    links = traffic.links() | chain.links

    def carried(*refs):
        groups = []
        for size in sizes:
            groups.append(refs[:size])
            refs = refs[size:]
        ins, sources, chain_in, outs, targets, chain_out, held, chain_held = groups
        ends = (sources, targets)
        step = pl.program_id(0)
        pl.when(step == 0)(lambda: greet(links))
        arrived = set()
        for which, at in enumerate(traffic.steps):

            @pl.when(step == at)
            def _():
                traffic.start(which, ends, *refs, arrived)

        for at, action in chain.actions[:-1]:

            @pl.when(step == at)
            def _():
                action(*chain_in, *chain_out, *chain_held)

        body(*ins, *outs, *held)

        @pl.when(step == grid[0] - 1)
        def _():
            if traffic.count():
                traffic.finish(ends, *refs, arrived)
            if chain.actions:
                chain.actions[-1][1](*chain_in, *chain_out, *chain_held)

    count = traffic.count()
    semaphores = [pltpu.SemaphoreType.DMA((count,))] * 2 if count else []
    outs = pl.pallas_call(
        carried,
        grid=grid,
        in_specs=list(in_specs) + [anywhere] * n_src + list(chain.in_specs),
        out_specs=list(out_specs) + [anywhere] * n_dst + list(chain.out_specs),
        out_shape=list(out_shape) + list(traffic.targets) + list(chain.out_shape),
        scratch_shapes=list(scratch) + list(chain.scratch) + semaphores,
        compiler_params=pltpu.CompilerParams(collective_id=ident, has_side_effects=True),
        cost_estimate=cost,
        name=name,
    )(*args, *traffic.sources, *chain.args)
    return outs[:n_out], outs[n_out : n_out + n_dst], outs[n_out + n_dst :]


COT_PATHS = {
    (0, 0, 1): ("y", (0, 0, 0), -1.500),
    (0, 1, 0): ("x", (0, 0, 0), 3.002),
    (0, 1, 1): ("x", (0, 0, 1), 2.463),
    (1, 0, 0): ("near", (0, 0, 0), 5.503),
    (1, 0, 1): ("y", (1, 0, 0), 0.791),
    (1, 1, 0): ("near", (0, 1, 0), 0.934),
    (1, 1, 1): ("x", (1, 0, 1), 1.171),
    (2, 0, 0): ("reach", (0, 0, 0), 2.419),
    (2, 0, 1): ("y", (2, 0, 0), 2.680),
    (2, 1, 0): ("reach", (0, 1, 0), 0.624),
    (2, 1, 1): ("x", (2, 0, 1), 5.712),
    (3, 0, 0): ("inner", (1, 0, 0), 0.725),
    (3, 0, 1): ("y", (3, 0, 0), 2.905),
    (3, 1, 0): ("x", (3, 0, 0), 4.267),
    (3, 1, 1): ("x", (3, 0, 1), 3.366),
}
ROW_PATHS = {
    (0, 0, 1): ("y", (0, 0, 0), -1.400),
    (0, 1, 0): ("x", (0, 0, 0), 0.507),
    (0, 1, 1): ("x", (0, 0, 1), 3.006),
    (1, 0, 0): ("near", (0, 0, 0), 4.270),
    (1, 0, 1): ("y", (1, 0, 0), 1.765),
    (1, 1, 0): ("near", (0, 1, 0), 5.532),
    (1, 1, 1): ("x", (1, 0, 1), 0.781),
    (2, 0, 0): ("inner", (0, 0, 0), 2.116),
    (2, 0, 1): ("y", (2, 0, 0), 1.823),
    (2, 1, 0): ("x", (2, 0, 0), 0.695),
    (2, 1, 1): ("y", (2, 1, 0), 3.141),
    (3, 0, 0): ("reach", (1, 0, 0), 3.737),
    (3, 0, 1): ("y", (3, 0, 0), 2.332),
    (3, 1, 0): ("inner", (1, 1, 0), 3.735),
    (3, 1, 1): ("x", (3, 0, 1), 4.908),
}
FAR_FIRST = {(0, 0, 1): ("y", (0, 0, 0), -2.0)}
FAR_LAST = {(0, 0, 1): ("y", (0, 0, 0), 5.198)}


class Network:
    def __init__(self):
        self.have, self.hops, self.weight, self.pieces = {}, {}, {}, {}

    def offer(self, name, array, hops, weight=1):
        self.hops[name], self.weight[name] = hops, weight
        self.pieces[name] = array.shape[0]
        for p in range(array.shape[0]):
            self.have[name, (0, 0, 0), p] = (array, p)

    def order(self, item):
        name, block, p = item
        return self.hops[name][block][2], block, p

    def missing(self):
        return [
            (name, block, p)
            for name in self.hops
            for block in self.hops[name]
            for p in range(self.pieces[name])
            if (name, block, p) not in self.have
        ]

    def complete(self, name, block):
        return all((name, block, p) in self.have for p in range(self.pieces[name]))

    def plan(self, room, steps, times):
        waiting = sorted(self.missing(), key=self.order)
        landed, rounds, going = {}, [[] for _ in steps], {}
        free = dict.fromkeys(("x", "y", "near", "inner"), 0.0)
        uses = {"reach": (("inner", 2), ("near", 1))}
        lag = 0.4

        def fill(link, now, weight, horizon):
            spans = [(on, max(free[on], now), n * weight) for on, n in uses.get(link, ((link, 1),))]
            if weight and any(begin >= horizon or begin + length > room + 0.01 for _, begin, length in spans):
                return None
            for on, begin, length in spans:
                if length:
                    free[on] = begin + length
            return max(begin + length for _, begin, length in spans) + lag

        for r, now in enumerate(times):
            horizon = times[r + 1] + 0.5 if r + 1 < len(times) else room
            for item in [i for i, (_, at) in going.items() if at <= now]:
                done = fill("near", now, self.weight[item[0]], horizon)
                if done is not None:
                    rounds[r].append(("outward", item, item))
                    landed[item] = done
                    del going[item]
            for item in waiting:
                name, block, p = item
                if item in landed or item in going:
                    continue
                link, source, _ = self.hops[name][block]
                source = (name, source, p)
                if source not in self.have and landed.get(source, now + 1) > now:
                    continue
                if link == "inner":
                    left = room - max(free["near"], now + 1) - sum(self.weight[i[0]] for i in going)
                    if r + 1 >= len(times) or left < 1 + self.weight[name] or times[-1] < now + self.weight[name] + lag:
                        continue
                done = fill(link, now, self.weight[name], horizon)
                if done is None:
                    continue
                if link == "reach":
                    rounds[r] += [("inner", source, item), ("skip", source, item)]
                else:
                    rounds[r].append((link, source, item))
                if link == "inner":
                    going[item] = (r, done)
                else:
                    landed[item] = done
        for item in list(going):
            rounds[-1].append(("outward", item, item))
            landed[item] = room
        sources, targets, homes = [], [], {}
        for name, block, p in sorted(landed):
            homes.setdefault((name, block), []).append(p)
        order = list(homes)
        for name, block in order:
            model = self.have[name, (0, 0, 0), 0][0]
            targets.append(jax.ShapeDtypeStruct((len(homes[name, block]),) + model.shape[1:], model.dtype))

        def home(item):
            name, block, p = item
            return order.index((name, block)), homes[name, block].index(p)

        def origin(item):
            if item in landed:
                return (1,) + home(item)
            array, at = self.have[item]
            for k, known in enumerate(sources):
                if known is array:
                    return 0, k, at
            sources.append(array)
            return 0, len(sources) - 1, at

        moves = []
        for chosen in rounds:
            spans = []
            for link, source, item in sorted(chosen, key=lambda c: (c[0] not in ("outward", "inner"), *c)):
                a, b = origin(source), home(item)
                if spans:
                    link_, a_, b_, n = spans[-1]
                    if link_ == link and a_[:2] == a[:2] and b_[0] == b[0] and a[2] == a_[2] + n and b[1] == b_[1] + n:
                        spans[-1] = (link, a_, b_, n + 1)
                        continue
                spans.append((link, a, b, 1))
            flat = [m for made in moves for m in made]
            placed = []
            for link, a, b, n in spans:
                needs = [
                    k
                    for k, m in enumerate(flat)
                    if a[0] == 1 and m.home[0] == a[1] and m.home[1] < a[2] + n and a[2] < m.home[1] + m.size
                ]
                placed.append(self.move(link, a, b, n, needs))
            moves.append(placed)
        while moves and not moves[-1]:
            moves.pop()
        traffic = Traffic(sources, targets, moves, steps[: len(moves)])
        return traffic, (order, homes)

    @staticmethod
    def move(link, origin, home, count, needs):
        def source(refs):
            return refs[origin[0]][origin[1]].at[pl.ds(origin[2], count)]

        def target(refs):
            return refs[1][home[0]].at[pl.ds(home[1], count)]

        made = Move(link, source, target, needs)
        made.home, made.size = home, count
        return made

    def land(self, plan, arrays):
        order, homes = plan
        for key, array in zip(order, arrays):
            for at, p in enumerate(homes[key]):
                self.have[key[0], key[1], p] = (array, at)

    def block(self, name, block):
        return [self.have[name, block, p] for p in range(self.pieces[name])]


def evenly(room, steps, length, every=1):
    chosen = list(range(0, steps, every))
    return room, chosen, [step * length for step in chosen]


def gathering(room, senders, extra):
    busy = 2 * senders * 0.45
    times = [0.45 * step for step in range(2 * senders)]
    times += [busy + (step + 1) * max(0.5, room - busy) / (extra + 1) for step in range(extra)]
    return room, list(range(2 * senders + extra)), times


def standardise(values):
    average = jnp.mean(values, axis=-1, keepdims=True)
    centred = values - average
    variance = jnp.mean(centred * centred, axis=-1, keepdims=True)
    scale = lax.rsqrt(variance + 1e-06)
    return centred * scale, scale


def prep_body(count_ref, cap_ref, tok_ref, cot_ref, route_ref, tok_out, cot_out, route_out, ids_out, load_out, wide, narrow):
    pl.when(pl.program_id(0) == 0)(
        lambda: prep_rows(
            count_ref, cap_ref, tok_ref, cot_ref, route_ref, tok_out, cot_out, route_out, ids_out, load_out, wide, narrow
        )
    )


def prep_rows(count_ref, cap_ref, tok_ref, cot_ref, route_ref, tok_out, cot_out, route_out, ids_out, load_out, wide, narrow):
    images = tok_out.shape[0]
    total = tok_ref.shape[0]
    alive_images = count_ref[0]
    real = iota((PAD, 1), 0) < IMG_TOK

    def split(source, image):
        return source[pl.ds(image * IMG_TOK, PAD), :]

    wide[...] = jnp.zeros_like(wide)
    narrow[...] = jnp.zeros_like(narrow)
    wide[pl.ds(0, total), :] = tok_ref[...].astype(F32)
    for image in range(images):
        tok_out[image] = jnp.where(real, split(wide, image), 0.0).astype(BF16)
    wide[pl.ds(0, total), :] = cot_ref[...].astype(F32)
    narrow[pl.ds(0, total), :] = route_ref[...]
    routes = []
    lives = []
    for image in range(images):
        live = real & (image < alive_images)
        cot_out[image] = jnp.where(live, split(wide, image), 0.0).astype(BF16)
        picked = split(narrow, image)
        route_out[image] = picked
        routes.append(picked)
        lives.append(jnp.where(live, 1, 0))
    routes = jnp.concatenate(routes, axis=0)
    live = jnp.concatenate(lives, axis=0) > 0
    rows = images * PAD
    lane = iota((rows, 128), 1)
    first = (lane == routes[:, 0:1]) & live
    second = (lane == routes[:, 1:2] + EXPERTS) & live
    hot = jnp.where(first | second, 1.0, 0.0)
    below = jnp.where(iota((rows, rows), 0) > iota((rows, rows), 1), 1.0, 0.0).astype(BF16)
    before = dot(below, hot.astype(BF16))
    totals = jnp.sum(hot, axis=0, keepdims=True)
    place_one = jnp.sum(jnp.where(first, before, 0.0), axis=1, keepdims=True)
    place_two = jnp.sum(jnp.where(second, before, 0.0), axis=1, keepdims=True) + jnp.sum(
        jnp.where(lane == routes[:, 1:2], totals, 0.0), axis=1, keepdims=True
    )
    limit = cap_ref[0].astype(F32)
    keep_one = live & (place_one < limit)
    keep_two = live & (place_two < limit)
    slots = jnp.where(lane == 0, jnp.where(keep_one, routes[:, 0:1].astype(F32), -1.0), 0.0)
    slots = jnp.where(lane == 1, jnp.where(keep_one, place_one, 0.0), slots)
    slots = jnp.where(lane == 2, jnp.where(keep_two, routes[:, 1:2].astype(F32), -1.0), slots)
    slots = jnp.where(lane == 3, jnp.where(keep_two, place_two, 0.0), slots)
    for image in range(images):
        ids_out[image] = jnp.transpose(slots[image * PAD : (image + 1) * PAD])[0:8]
    lanes = iota((1, 128), 1)
    tokens_alive = (alive_images * IMG_TOK).astype(F32)
    load_out[0] = jnp.broadcast_to(jnp.where(lanes == 64, tokens_alive, totals), (8, 128))


def weight_traffic(wide, tall):
    def rows(array):
        half = array.shape[0] // 2
        return pl.ds(pl.multiple_of((lax.axis_index("rep") % 2) * half, 8), half)

    def fetch(at, array):
        return Move("y", lambda refs: refs[0][at].at[rows(array)], lambda refs: refs[1][at].at[rows(array)])

    def pass_on(at, array):
        there = lambda refs: refs[1][at].at[rows(array)]
        return Move("core", there, there, [at])

    arrays = (wide, tall)
    targets = [jax.ShapeDtypeStruct(a.shape, a.dtype) for a in arrays]
    rounds = [[make(at, a) for at, a in enumerate(arrays)] for make in (fetch, pass_on)]
    return Traffic(list(arrays), targets, rounds, [0, 1])


def prepare(tokens, cotangent, routes, image_count, capacity, wide, tall, ident):
    total, width = tokens.shape
    images = total // IMG_TOK
    shapes = [
        jax.ShapeDtypeStruct((images, PAD, width), BF16),
        jax.ShapeDtypeStruct((images, PAD, width), BF16),
        jax.ShapeDtypeStruct((images, PAD, 2), jnp.int32),
        jax.ShapeDtypeStruct((images, 8, PAD), F32),
        jax.ShapeDtypeStruct((1, 8, 128), F32),
    ]
    return run(
        prep_body,
        (image_count, capacity, tokens, cotangent, routes),
        [scalar_spec(), scalar_spec()] + [resident(a.shape) for a in (tokens, cotangent, routes)],
        [resident(a.shape) for a in shapes],
        shapes,
        grid=(2,),
        scratch=[pltpu.VMEM((1000, width), F32), pltpu.VMEM((1000, 2), jnp.int32)],
        cost=pl.CostEstimate(flops=300_000_000, bytes_accessed=6_000_000, transcendentals=0),
        name="prepare",
        traffic=weight_traffic(wide, tall),
        ident=ident,
    )


def place_halves(own, far, both):
    mine = lax.axis_index("fsdp")
    both[mine] = own[...]
    both[1 - mine] = far[...]


def vectors(wide_ref):
    return jnp.concatenate([wide_ref[0, 256:272, :256], wide_ref[1, 256:272, :256]], axis=1).astype(F32)


def front_body(
    count_ref, tok_ref, ids_ref, route_ref, wide_own, wide_far, tall_own, tall_far,
    packed_ref, prob_ref, mixed_ref, middle_ref, second_ref, soft_ref, sum_ref, wide_ref, tall_ref,
):
    @pl.when(pl.program_id(0) == 0)
    def _():
        sum_ref[...] = jnp.zeros_like(sum_ref)
        place_halves(wide_own, wide_far, wide_ref)
        place_halves(tall_own, tall_far, tall_ref)

    width = tok_ref.shape[-1]
    vec = vectors(wide_ref)
    inputs = tok_ref[0].astype(F32)
    normed = (standardise(inputs)[0] * vec[0:1] + vec[1:2]).astype(BF16)
    qkv = wide_ref[:, :256, :].reshape(width, 3 * width)
    raw = dot(normed, qkv)
    packed_ref[0, :, :width] = (raw[:, :width] + vec[2:3]).astype(BF16)
    packed_ref[0, :, width : 2 * width] = raw[:, width : 2 * width].astype(BF16)
    packed_ref[0, :, 2 * width :] = (raw[:, 2 * width :] + vec[3:4]).astype(BF16)
    low_lanes = iota((PAD, 128), 1) < HEAD_DIM
    real_key = iota((PAD, PAD), 1) < IMG_TOK
    for pair in range(HEADS // 2):
        at = pair * 128
        query = packed_ref[0, :, at : at + 128] * jnp.asarray(HEAD_DIM**-0.5, BF16)
        keys = packed_ref[0, :, width + at : width + at + 128]
        valued = packed_ref[0, :, 2 * width + at : 2 * width + at + 128]
        got = []
        for side in range(2):
            own = low_lanes if side == 0 else ~low_lanes
            scores = dot_cols(jnp.where(own, query, jnp.zeros_like(query)), keys)
            scores = jnp.where(real_key, scores, -1e30)
            raised = jnp.exp(scores - jnp.max(scores, axis=-1, keepdims=True))
            weights = (raised / jnp.sum(raised, axis=-1, keepdims=True)).astype(BF16)
            prob_ref[0, 2 * pair + side] = weights
            got.append(dot(weights, valued))
        mixed_ref[0, :, at : at + 128] = jnp.where(low_lanes, got[0], got[1]).astype(BF16)
    out_full = tall_ref[:, :, :width].reshape(width, width)
    router = tall_ref[:, :, width : width + 128].reshape(width, 128)
    middle = inputs + dot(mixed_ref[0], out_full) + vec[4:5]
    middle_ref[0] = middle
    second = standardise(middle)[0] * vec[5:6] + vec[6:7]
    lane = iota((PAD, 128), 1)
    logits = jnp.where(lane < EXPERTS, dot(second.astype(BF16), router), -1e30)
    soft = jnp.exp(logits - jnp.max(logits, axis=-1, keepdims=True))
    soft = soft / jnp.sum(soft, axis=-1, keepdims=True)
    route = route_ref[0]
    pick_one = jnp.sum(jnp.where(lane == route[:, 0:1], soft, 0.0), axis=-1, keepdims=True)
    pick_two = jnp.sum(jnp.where(lane == route[:, 1:2], soft, 0.0), axis=-1, keepdims=True)
    both = pick_one + pick_two
    live = (iota((PAD, 1), 0) < IMG_TOK) & (pl.program_id(0) < count_ref[0])
    alive = jnp.where(live, 1.0, 0.0)
    sum_ref[0] += jnp.broadcast_to(jnp.sum(soft * alive, axis=0, keepdims=True), (8, 128))
    soft = jnp.where(lane == EXPERTS + 4, pick_one / both, soft)
    soft = jnp.where(lane == EXPERTS + 5, pick_two / both, soft)
    soft_ref[0] = soft
    gates = jnp.transpose(soft)[EXPERTS : EXPERTS + 8]
    line = iota((8, PAD), 0)
    meta = jnp.where((line == 4) | (line == 5), gates, ids_ref[0])
    meta = jnp.concatenate([meta, jnp.zeros((8, width - PAD), F32)], axis=1)
    second_ref[0] = jnp.concatenate([second[: PAD - 8], meta], axis=0).astype(BF16)


def front(count, tok, ids, routes, wide, tall, traffic, ident):
    images, _, width = tok.shape
    shape = jax.ShapeDtypeStruct
    return run(
        front_body,
        (count, tok, ids, routes, *wide, *tall),
        [scalar_spec(), by_image(PAD, width), by_image(8, PAD), by_image(PAD, 2)]
        + [resident(wide[0].shape)] * 2
        + [resident(tall[0].shape)] * 2,
        [
            by_image(PAD, 3 * width),
            by_image(HEADS, PAD, PAD),
            by_image(PAD, width),
            by_image(PAD, width),
            by_image(PAD, width),
            by_image(PAD, 128),
            resident((1, 8, 128)),
        ],
        [
            shape((images, PAD, 3 * width), BF16),
            shape((images, HEADS, PAD, PAD), BF16),
            shape((images, PAD, width), BF16),
            shape((images, PAD, width), F32),
            shape((images, PAD, width), BF16),
            shape((images, PAD, 128), F32),
            shape((1, 8, 128), F32),
        ],
        grid=(images,),
        scratch=[pltpu.VMEM((2,) + wide[0].shape, BF16), pltpu.VMEM((2,) + tall[0].shape, BF16)],
        cost=pl.CostEstimate(flops=6_000_000_000, bytes_accessed=16_000_000, transcendentals=2_000_000),
        name="front",
        traffic=traffic,
        ident=ident,
    )


def slot_lines(meta):
    return meta[0:1] * CAP + meta[1:2], meta[2:3] * CAP + meta[3:4]


def gather_body(base_ref, *refs, parts, senders):
    arrays, (row_out, grad_out, rows, lines) = refs[:parts], refs[parts:]
    experts, _, cap, width = row_out.shape
    slots = experts * cap
    tokens = rows.shape[0]
    step = pl.program_id(0)
    for k, pair in enumerate(senders):
        for kind, pieces in enumerate(pair):

            @pl.when(step == 2 * k + kind)
            def _():
                for image, (at, position) in enumerate(pieces):
                    value = arrays[at][position]
                    rows[image * PAD : (image + 1) * PAD, :] = value
                    if kind == 0:
                        lines[image] = value[PAD - 16 :, :PAD].astype(F32)[8:]

    @pl.when(step < 2 * len(senders))
    def _():
        meta = jnp.concatenate([lines[image] for image in range(lines.shape[0])], axis=1)
        one, two = slot_lines(meta)
        gated = step % 2 == 1
        weight_one = jnp.where(gated, meta[4:5], 1.0)
        weight_two = jnp.where(gated, meta[5:6], 1.0)
        slot = (iota((slots, tokens), 0) + base_ref[0]).astype(F32)
        pick = jnp.where(slot == one, weight_one, 0.0) + jnp.where(slot == two, weight_two, 0.0)
        got = dot(pick.astype(BF16), rows[...]).astype(BF16).reshape(experts, 1, cap, width)

        @pl.when(step % 2 == 0)
        def _():
            row_out[...] = got

        @pl.when(step % 2 == 1)
        def _():
            grad_out[...] = got


def gather(base, experts, senders, extra, traffic, ident, chain=None):
    arrays, table = [], []
    for pair in senders:
        table.append([])
        for pieces in pair:
            table[-1].append([])
            for array, position in pieces:
                at = next((k for k, known in enumerate(arrays) if known is array), len(arrays))
                if at == len(arrays):
                    arrays.append(array)
                table[-1][-1].append((at, position))
    width = arrays[0].shape[-1]
    images = len(table[0][0])
    tokens = images * PAD
    count = len(senders)
    shape = jax.ShapeDtypeStruct((experts, count, CAP, width), BF16)
    return run(
        lambda *refs: gather_body(*refs, parts=len(arrays), senders=table),
        (base, *arrays),
        [scalar_spec()]
        + [pl.BlockSpec(a.shape, lambda d: (0, 0, 0), pipeline_mode=pl.Buffered(1)) for a in arrays],
        [pl.BlockSpec((experts, 1, CAP, width), lambda d: (0, jnp.minimum(d // 2, count - 1), 0, 0))] * 2,
        [shape, shape],
        grid=(2 * count + extra,),
        scratch=[pltpu.VMEM((tokens, width), BF16), pltpu.VMEM((images, 8, PAD), F32)],
        cost=pl.CostEstimate(
            flops=4 * count * experts * CAP * tokens * width,
            bytes_accessed=4 * count * (tokens + experts * CAP) * width,
            transcendentals=0,
        ),
        name="gather",
        traffic=traffic,
        chain=chain,
        ident=ident,
    )


def expert_body(row_own, row_far, grad_own, grad_far, in_ref, in_bias_ref, out_ref, out_bias_ref, made_own, made_far, back_own, back_far):
    cap, width = row_own.shape[2:]
    hidden = in_ref.shape[2]
    rows = jnp.concatenate([row_own[0, 0], row_far[0, 0]], axis=0)
    grads = jnp.concatenate([grad_own[0, 0], grad_far[0, 0]], axis=0)
    made = jnp.zeros((2 * cap, width), F32)
    back = jnp.zeros((2 * cap, width), F32)
    chunk = 512
    for at in range(0, hidden, chunk):
        first = in_ref[0, :, at : at + chunk]
        second = out_ref[0, at : at + chunk, :]
        raised = dot(rows, first) + in_bias_ref[0, :, at : at + chunk].astype(F32)
        active, slope = gelu_pair(raised)
        made += dot(active.astype(BF16), second)
        draised = (dot_cols(grads, second) * slope).astype(BF16)
        back += dot_cols(draised, first)
    made = (made + out_bias_ref[0].astype(F32)).astype(BF16)
    back = back.astype(BF16)
    made_own[0], made_far[0] = made[:cap], made[cap:]
    back_own[0], back_far[0] = back[:cap], back[cap:]


def expert_layer(own, far, first, first_bias, second, second_bias, chain, traffic, ident):
    experts, _, cap, width = own[0].shape
    hidden = first.shape[2]
    rows = pl.BlockSpec((1, 1, cap, width), lambda e: (e, 0, 0, 0))
    out = pl.BlockSpec((1, cap, width), lambda e: (e, 0, 0))
    return run(
        expert_body,
        (
            own[0],
            far[0],
            own[1],
            far[1],
            first,
            first_bias.reshape(experts, 1, hidden),
            second,
            second_bias.reshape(experts, 1, width),
        ),
        [rows] * 4 + [by_image(width, hidden), by_image(1, hidden), by_image(hidden, width), by_image(1, width)],
        [out] * 4,
        [jax.ShapeDtypeStruct((experts, cap, width), BF16)] * 4,
        grid=(experts,),
        cost=pl.CostEstimate(
            flops=16 * experts * cap * width * hidden,
            bytes_accessed=4 * experts * width * hidden,
            transcendentals=2 * experts * cap * hidden,
        ),
        name="expert_layer",
        traffic=traffic,
        chain=chain,
        ident=ident,
    )


def combine_body(base_ref, rows, cot, made_ref, back_ref, sum_ref, row_ref, gate_ref):
    experts, cap, width = made_ref.shape
    slots = experts * cap
    meta = jnp.transpose(rows[PAD - 16 :, :PAD].astype(F32)[8:])
    slot = (iota((PAD, slots), 1) + base_ref[0]).astype(F32)
    one = jnp.where(slot == meta[:, 0:1] * CAP + meta[:, 1:2], 1.0, 0.0).astype(BF16)
    two = jnp.where(slot == meta[:, 2:3] * CAP + meta[:, 3:4], 1.0, 0.0).astype(BF16)
    made = made_ref[...].reshape(slots, width)
    made_one = dot(one, made)
    made_two = dot(two, made)
    sum_ref[0] = (meta[:, 4:5] * made_one + meta[:, 5:6] * made_two).astype(BF16)
    row_ref[0] = dot(one + two, back_ref[...].reshape(slots, width)).astype(BF16)
    cot = cot.astype(F32)
    grad_one = jnp.sum(cot * made_one, axis=1, keepdims=True)
    grad_two = jnp.sum(cot * made_two, axis=1, keepdims=True)
    lane = iota((PAD, 128), 1)
    wide = jnp.where(lane == 0, grad_one, jnp.where(lane == 1, grad_two, 0.0))
    gate_ref[0] = jnp.transpose(wide)[0:8]


def by_piece(pieces, *shape):
    arrays, first = [], []
    for image, (array, position) in enumerate(pieces):
        if not arrays or arrays[-1] is not array:
            arrays.append(array)
            first.append((image, position))
    specs = []
    for array, (image, position) in zip(arrays, first):

        def index(i, *_, image=image, position=position, last=array.shape[0] - 1):
            return (jnp.clip(i - image + position, 0, last),) + (0,) * len(shape)

        specs.append(pl.BlockSpec((1,) + shape, index))

    def read(refs):
        value = refs[0][0]
        for ref, (image, _) in zip(refs[1:], first[1:]):
            value = jnp.where(pl.program_id(0) >= image, ref[0], value)
        return value

    return arrays, specs, read


def combine(base, rows, cots, made, back, traffic, ident):
    width = made.shape[-1]
    images = len(rows)
    experts, cap, _ = made.shape
    row_arrays, row_specs, read_rows = by_piece(rows, PAD, width)
    cot_arrays, cot_specs, read_cots = by_piece(cots, PAD, width)
    split = len(row_arrays)

    def body(base_ref, made_ref, back_ref, *refs):
        inputs, outs = refs[: split + len(cot_arrays)], refs[split + len(cot_arrays) :]
        combine_body(base_ref, read_rows(inputs[:split]), read_cots(inputs[split:]), made_ref, back_ref, *outs)

    return run(
        body,
        (base, made, back, *row_arrays, *cot_arrays),
        [scalar_spec(), resident(made.shape), resident(back.shape), *row_specs, *cot_specs],
        [by_image(PAD, width), by_image(PAD, width), by_image(8, PAD)],
        [
            jax.ShapeDtypeStruct((images, PAD, width), BF16),
            jax.ShapeDtypeStruct((images, PAD, width), BF16),
            jax.ShapeDtypeStruct((images, 8, PAD), F32),
        ],
        grid=(images,),
        cost=pl.CostEstimate(
            flops=6 * images * PAD * experts * cap * width, bytes_accessed=6_000_000, transcendentals=0
        ),
        name="combine",
        traffic=traffic,
        ident=ident,
    )


def norm_back(grads, hat, scale, gain):
    scaled = grads * gain
    inner = jnp.mean(scaled * hat, axis=-1, keepdims=True)
    return scale * (scaled - jnp.mean(scaled, axis=-1, keepdims=True) - hat * inner)


def column_sum(values):
    return jnp.sum(values, axis=0, keepdims=True)


def finish_body(
    count_ref, tok_ref, cot_ref, packed_ref, prob_ref, mixed_ref, middle_ref, second_ref, soft_ref, route_ref,
    row_own, row_far, gate_own, gate_far, aux_ref,
    wide_own, wide_far, tall_own, tall_far, dtok_ref, pack_ref,
    dpacked, wide_ref, tall_ref, dqkv_ref, dout_ref, drouter_ref, dvec_ref,
):
    image = pl.program_id(0)
    width = tok_ref.shape[-1]

    @pl.when(image == 0)
    def _():
        place_halves(wide_own, wide_far, wide_ref)
        place_halves(tall_own, tall_far, tall_ref)

    vec = vectors(wide_ref)
    images = dtok_ref.shape[0] // IMG_TOK

    @pl.when(image == 0)
    def _():
        for ref in (dqkv_ref, dout_ref, drouter_ref, dvec_ref):
            ref[...] = jnp.zeros_like(ref)

    real = iota((PAD, 1), 0) < IMG_TOK
    alive = jnp.where(real & (image < count_ref[0]), 1.0, 0.0)
    middle = middle_ref[0]
    upstream = cot_ref[0].astype(F32)
    soft = soft_ref[0]
    route = route_ref[0]
    lane = iota((PAD, 128), 1)
    gate_grads = jnp.transpose(gate_own[0] + gate_far)
    push = (gate_grads[:, 0:1] - gate_grads[:, 1:2]) * soft[:, EXPERTS + 4 : EXPERTS + 5] * soft[:, EXPERTS + 5 : EXPERTS + 6]
    soft = jnp.where(lane < EXPERTS, soft, 0.0)
    aux = aux_ref[...] * alive
    dlogits = soft * (aux - jnp.sum(soft * aux, axis=-1, keepdims=True))
    dlogits += jnp.where(lane == route[:, 0:1], push, 0.0) - jnp.where(lane == route[:, 1:2], push, 0.0)
    dlogits = dlogits.astype(BF16)
    second = second_ref[0]
    router = tall_ref[:, :, width : width + 128].reshape(width, 128)
    drouter_ref[...] += dot_rows(second, dlogits)
    dsecond = dot_cols(dlogits, router) + (row_own[0].astype(F32) + row_far.astype(F32))
    hat, scale = standardise(middle)
    dmiddle = upstream + norm_back(dsecond, hat, scale, vec[5:6])
    dattn = dmiddle.astype(BF16)
    dvec_ref[EXPERTS + 4 : EXPERTS + 5] += column_sum(dattn.astype(F32))
    dvec_ref[EXPERTS + 5 : EXPERTS + 6] += column_sum(dsecond * hat)
    dvec_ref[EXPERTS + 6 : EXPERTS + 7] += column_sum(dsecond)
    dout_ref[...] += dot_rows(mixed_ref[0], dattn)
    out_full = tall_ref[:, :, :width].reshape(width, width)
    dmixed = dot_cols(dattn, out_full).astype(BF16)
    low_lanes = iota((PAD, 128), 1) < HEAD_DIM
    root = HEAD_DIM**-0.5
    for pair in range(HEADS // 2):
        at = pair * 128
        query = packed_ref[0, :, at : at + 128]
        keys = packed_ref[0, :, width + at : width + at + 128]
        valued = packed_ref[0, :, 2 * width + at : 2 * width + at + 128]
        grads = dmixed[:, at : at + 128]
        parts = []
        for side in range(2):
            own = low_lanes if side == 0 else ~low_lanes
            weights = prob_ref[0, 2 * pair + side]
            dweights = dot_cols(jnp.where(own, grads, jnp.zeros_like(grads)), valued)
            exact = weights.astype(F32)
            inner = jnp.sum(dweights * exact, axis=-1, keepdims=True)
            dscores = (exact * (dweights - inner)).astype(BF16)
            parts.append((dot(dscores, keys), dot_rows(dscores, query), dot_rows(weights, grads)))
        for third, factor in ((0, root), (1, root), (2, 1.0)):
            both = jnp.where(low_lanes, parts[0][third], parts[1][third]) * factor
            dpacked[:, third * width + at : third * width + at + 128] = both.astype(BF16)
    inputs = tok_ref[0].astype(F32)
    hat, scale = standardise(inputs)
    normed = (hat * vec[0:1] + vec[1:2]).astype(BF16)
    packed_grads = dpacked[...]
    dqkv_ref[...] += dot_rows(normed, packed_grads)
    dvec_ref[EXPERTS + 2 : EXPERTS + 3] += column_sum(packed_grads[:, :width].astype(F32))
    dvec_ref[EXPERTS + 3 : EXPERTS + 4] += column_sum(packed_grads[:, 2 * width :].astype(F32))
    qkv = wide_ref[:, :256, :].reshape(width, 3 * width)
    dnormed = dot_cols(packed_grads, qkv)
    dvec_ref[EXPERTS + 0 : EXPERTS + 1] += column_sum(dnormed * hat)
    dvec_ref[EXPERTS + 1 : EXPERTS + 2] += column_sum(dnormed)
    dtokens = dmiddle + norm_back(dnormed, hat, scale, vec[0:1])
    for k in range(images):

        @pl.when(image == k)
        def _():
            dtok_ref[pl.ds(k * IMG_TOK, IMG_TOK), :] = dtokens[:IMG_TOK]

    @pl.when(image == images - 1)
    def _():
        lines = jnp.transpose(dvec_ref[...])
        part = width // 8
        for owner in range(2):
            for half in range(2):
                for quarter in range(2):
                    at = ((owner * 2 + half) * 2 + quarter) * part
                    rows = slice(at, at + part)
                    spot = pack_ref.at[owner, half, quarter]
                    spot[:, : 3 * width] = dqkv_ref[rows].astype(BF16)
                    spot[:, 3 * width : 4 * width] = dout_ref[rows].astype(BF16)
                    spot[:, 4 * width :] = (drouter_ref[rows] + lines[rows]).astype(BF16)


def finish(count, tok, cot, saved, routes, row_own, row_far, gate_own, gate_far, aux, wide, tall, total, traffic, ident):
    images, _, width = tok.shape
    packed, prob, mixed, middle, second, soft = saved
    shape = jax.ShapeDtypeStruct
    tile = by_image(PAD, width)
    row_arrays, row_specs, read_rows = by_piece(row_far, PAD, width)
    gate_arrays, gate_specs, read_gates = by_piece(gate_far, 8, PAD)
    extra = len(row_arrays) + len(gate_arrays)

    def body(*refs):
        pieces, refs = refs[:extra], list(refs[extra:])
        refs[11:11] = [read_rows(pieces[: len(row_arrays)])]
        refs[13:13] = [read_gates(pieces[len(row_arrays) :])]
        finish_body(*refs)

    pack = (2, 2, 2, width // 8, 4 * width + 128)
    return run(
        body,
        (
            *row_arrays, *gate_arrays, count, tok, cot, packed, prob, mixed, middle, second, soft, routes,
            row_own, gate_own, aux, *wide, *tall,
        ),
        [
            *row_specs,
            *gate_specs,
            scalar_spec(),
            tile,
            tile,
            by_image(PAD, 3 * width),
            by_image(HEADS, PAD, PAD),
            tile,
            tile,
            tile,
            by_image(PAD, 128),
            by_image(PAD, 2),
            tile,
            by_image(8, PAD),
            resident((1, 128)),
            resident(wide[0].shape),
            resident(wide[0].shape),
            resident(tall[0].shape),
            resident(tall[0].shape),
        ],
        [resident((total, width)), resident(pack)],
        [shape((total, width), F32), shape(pack, BF16)],
        grid=(images,),
        scratch=[
            pltpu.VMEM((PAD, 3 * width), BF16),
            pltpu.VMEM((2,) + wide[0].shape, BF16),
            pltpu.VMEM((2,) + tall[0].shape, BF16),
            pltpu.VMEM((width, 3 * width), F32),
            pltpu.VMEM((width, width), F32),
            pltpu.VMEM((width, 128), F32),
            pltpu.VMEM((128, width), F32),
        ],
        cost=pl.CostEstimate(flops=12_000_000_000, bytes_accessed=24_000_000, transcendentals=0),
        name="finish",
        traffic=traffic,
        ident=ident,
    )


def add(left, right):
    return (left.astype(F32) + right.astype(F32)).astype(BF16)


class Exchange:
    def __init__(self, send, recv):
        self.send, self.recv = send, recv

    def at(self, index, link, source, target):
        move = Move(link, lambda _: source, lambda _: target)
        return move.roles(), move.copy(None, self.send.at[index], self.recv.at[index])


def begin(make):
    roles, copy = make()
    only_if(roles[0], copy.start)


def end(make):
    roles, copy = make()
    only_if(roles[0], copy.wait_send)
    only_if(roles[1], copy.wait_recv)


def sums_everywhere(load, soft_sum, steps):
    shape = (2,) + load.shape[1:]
    links = ("core", "y", "x", "near", "inner", "outward")

    def copies(load_ref, soft_ref, total, held, got, send, recv):
        made = Exchange(send, recv)
        return [
            lambda k=k, link=link: made.at(k, link, held.at[k], held.at[k] if link == "outward" else got.at[k])
            for k, link in enumerate(links)
        ]

    def first(*refs):
        load_ref, soft_ref, _, held = refs[:4]
        held[0, 0], held[0, 1] = load_ref[0], soft_ref[0]
        begin(copies(*refs)[0])

    def stage(k):
        def action(*refs):
            held, got = refs[3:5]
            end(copies(*refs)[k - 1])
            if links[k] == "outward":

                @pl.when(((lax.axis_index("rep") // 4) % 3) > 0)
                def _():
                    held[k] = held[k - 1] + got[k - 1]

            else:
                held[k] = held[k - 1] + got[k - 1]
            begin(copies(*refs)[k])

        return action

    def last(*refs):
        end(copies(*refs)[5])
        refs[2][...] = refs[3][5]

    return Chain(
        [load, soft_sum],
        [resident(load.shape)] * 2,
        [resident(shape)],
        [jax.ShapeDtypeStruct(shape, F32)],
        [pltpu.VMEM((6,) + shape, F32), pltpu.VMEM((5,) + shape, F32)] + [pltpu.SemaphoreType.DMA((6,))] * 2,
        {"core", "y", "x", "near", "inner"},
        list(zip(steps, [first] + [stage(k) for k in range(1, 6)])) + [(0, last)],
    )


def owner_sums(pack, steps):
    shape = pack.shape[2:]

    def first(pack_ref, part, near_in, half, far_in, send, recv):
        core = lax.axis_index("rep") % 2
        Exchange(send, recv).at(0, "core", pack_ref.at[:, 1 - core], near_in)[1].start()

    def second(pack_ref, part, near_in, half, far_in, send, recv):
        core, mine = lax.axis_index("rep") % 2, lax.axis_index("fsdp")
        Exchange(send, recv).at(0, "core", pack_ref.at[:, 1 - core], near_in)[1].wait()
        half[...] = add(pack_ref[:, core], near_in[...])
        Exchange(send, recv).at(1, "y", half.at[1 - mine], far_in)[1].start()

    def last(pack_ref, part, near_in, half, far_in, send, recv):
        mine = lax.axis_index("fsdp")
        Exchange(send, recv).at(1, "y", half.at[1 - mine], far_in)[1].wait()
        part[...] = add(half[mine], far_in[...])

    return Chain(
        [pack],
        [pl.BlockSpec(pack.shape, lambda *_: (0,) * 5, pipeline_mode=pl.Buffered(1))],
        [resident(shape)],
        [jax.ShapeDtypeStruct(shape, BF16)],
        [pltpu.VMEM((2,) + shape, BF16), pltpu.VMEM((2,) + shape, BF16), pltpu.VMEM(shape, BF16)]
        + [pltpu.SemaphoreType.DMA((2,))] * 2,
        {"core", "y"},
        [(0, first), (1, second), (steps, last)],
    )


def copy_sums(part, steps):
    shape = part.shape[1:]

    def copies(part_ref, total, x_in, held, near_in, line, inner_in, full, send, recv):
        device = lax.axis_index("rep")
        core, side = device % 2, (device // 2) % 2
        made = Exchange(send, recv)
        mine = full.at[core, side]
        plans = [
            ("x", part_ref.at[1 - side], x_in),
            ("near", held, near_in),
            ("inner", line, inner_in),
            ("outward", mine, mine),
            ("x", mine, mine),
            ("core", full.at[core], full.at[core]),
        ]
        return [lambda k=k, plan=plan: made.at(k, *plan) for k, plan in enumerate(plans)]

    def first(*refs):
        begin(copies(*refs)[0])

    def second(*refs):
        part_ref, total, x_in, held = refs[:4]
        steps = copies(*refs)
        end(steps[0])
        side = (lax.axis_index("rep") // 2) % 2
        held[...] = add(part_ref[side], x_in[...])
        begin(steps[1])

    def third(*refs):
        part_ref, total, x_in, held, near_in, line = refs[:6]
        steps = copies(*refs)
        end(steps[1])
        line[...] = add(held[...], near_in[...])
        begin(steps[2])

    def fourth(*refs):
        part_ref, total, x_in, held, near_in, line, inner_in, full = refs[:8]
        steps = copies(*refs)
        device = lax.axis_index("rep")
        middle = ((device // 4) % 3) > 0
        end(steps[2])

        @pl.when(middle)
        def _():
            full[device % 2, (device // 2) % 2] = add(line[...], inner_in[...])

        begin(steps[3])

    def fifth(*refs):
        steps = copies(*refs)
        end(steps[3])
        begin(steps[4])

    def sixth(*refs):
        steps = copies(*refs)
        end(steps[4])
        begin(steps[5])

    def last(*refs):
        total, full = refs[1], refs[7]
        end(copies(*refs)[5])
        total[...] = full[...]

    whole = (2, 2) + shape
    return Chain(
        [part],
        [resident(part.shape)],
        [resident(whole)],
        [jax.ShapeDtypeStruct(whole, BF16)],
        [pltpu.VMEM(shape, BF16)] * 5 + [pltpu.VMEM(whole, BF16)] + [pltpu.SemaphoreType.DMA((6,))] * 2,
        {"core", "x", "near", "inner"},
        list(zip(steps, (first, second, third, fourth, fifth, sixth))) + [(0, last)],
    )


def emit(count, middle, sum_own, sum_far, total):
    images, _, width = middle.shape
    far_arrays, far_specs, read_far = by_piece(sum_far, PAD, width)

    def body(count_ref, middle_ref, own_ref, *refs):
        far, (out_ref, held) = refs[:-2], refs[-2:]
        image = pl.program_id(0)
        live = (iota((PAD, 1), 0) < IMG_TOK) & (image < count_ref[0])
        both = own_ref[0].astype(F32) + read_far(far).astype(F32)
        result = jnp.where(live, 1.0, 0.0) * (middle_ref[0] + both)
        for k in range(images):

            @pl.when(image == k)
            def _():
                held[pl.ds(k * IMG_TOK, IMG_TOK), :] = result[:IMG_TOK]

        @pl.when(image == images - 1)
        def _():
            out_ref[...] = held[pl.ds(0, total), :].astype(BF16)

    tile = by_image(PAD, width)
    return run(
        body,
        (count, middle, sum_own, *far_arrays),
        [scalar_spec(), tile, tile, *far_specs],
        [resident((total, width))],
        [jax.ShapeDtypeStruct((total, width), BF16)],
        grid=(images,),
        scratch=[pltpu.VMEM((1000, width), F32)],
        cost=pl.CostEstimate(flops=2_000_000, bytes_accessed=6_000_000, transcendentals=0),
        name="emit",
    )[0][0]


def by_slice(
    tokens, cotangent, routes, image_count, capacity, norm1_gain, norm1_bias, w_qkv, bias_q, bias_v, w_out, bias_out,
    norm2_gain, norm2_bias, w_router, expert_in, expert_in_bias, expert_out, expert_out_bias,
):
    total, width = tokens.shape
    local = expert_in.shape[0]
    device = lax.axis_index("rep")
    mine = lax.axis_index("fsdp")
    core = device % 2
    small = jnp.stack([norm1_gain, norm1_bias, bias_q, bias_v, bias_out, norm2_gain, norm2_bias])
    small = jnp.pad(small, ((0, 9), (0, 3 * width - small.shape[1])))
    wide = jnp.concatenate([w_qkv, small], axis=0)
    tall = jnp.concatenate([w_out, jnp.pad(w_router, ((0, 0), (0, 128 - EXPERTS)))], axis=1)
    (tok, cot, route, ids, load), (wide_far, tall_far), _ = prepare(
        tokens, cotangent, routes, image_count, capacity, wide, tall, 0
    )
    wide, tall = (wide, wide_far), (tall, tall_far)
    base = (mine * (local * CAP)).reshape(1)
    net = Network()
    net.offer("C", cot, COT_PATHS)
    idents = iter(range(1, 32))

    def staged(kernel, *args, rounds):
        traffic, plan = net.plan(*rounds)
        outs, arrived, chained = kernel(*args, traffic, next(idents))
        net.land(plan, arrived)
        return (*outs, *chained)

    own, far = (0, 0, 0), (0, 0, 1)
    packed, prob, mixed, middle, second, soft, soft_sum = staged(
        front, image_count, tok, ids, route, wide, tall, rounds=evenly(4, 5, 0.68)
    )
    net.offer("S", second, ROW_PATHS)

    def sender(block):
        return net.block("S", block), net.block("C", block)

    slots = []
    taken = set()

    def take(blocks, room, extra):
        taken.update(blocks)
        outs = staged(
            gather, base, local, [sender(b) for b in blocks], extra, rounds=gathering(room, len(blocks), extra)
        )
        slots.append(outs)
        return outs

    def ready():
        return [b for b in COT_PATHS if b not in taken and net.complete("S", b) and net.complete("C", b)]

    slots_own = take([own], 6, 4)
    slots_far = take([far], 2, 1)
    made_own, made_far, back_own, back_far, sums = staged(
        expert_layer, slots_own, slots_far, expert_in, expert_in_bias, expert_out, expert_out_bias,
        sums_everywhere(load, soft_sum, (0, 2, 5, 8, 11, 13)),
        rounds=evenly(11, 16, 0.7, 2),
    )
    sum_far, drow_far, dgate_far = staged(
        combine, base, *sender(far), made_far, back_far, rounds=evenly(2, 5, 0.4, 2)
    )
    net.offer("D", drow_far, FAR_FIRST)
    net.offer("G", dgate_far, FAR_FIRST, 0)
    net.offer("M", sum_far, FAR_LAST)
    sum_own, drow_own, dgate_own = staged(
        combine, base, *sender(own), made_own, back_own, rounds=evenly(2, 5, 0.4, 2)
    )
    take(ready()[:2], 3, 1)
    loads, prob_total = sums[0, 0:1], sums[1, 0:1]
    live = loads[:, 64:65]
    share = (loads[:, :EXPERTS] + loads[:, EXPERTS : 2 * EXPERTS]) / (2.0 * live)
    aux = jnp.pad(EXPERTS * share / live, ((0, 0), (0, 128 - EXPERTS)))
    grad_tokens, pack = staged(
        finish, image_count, tok, cot, (packed, prob, mixed, middle, second, soft), route, drow_own,
        net.block("D", far), dgate_own, net.block("G", far), aux, wide, tall, total,
        rounds=evenly(7, 5, 1.5),
    )
    while True:
        now = ready()[:3]
        if not net.missing() and len(taken) + len(now) == 16:
            break
        take(now, 5, 2)
    traffic, plan = net.plan(0, [0], [0.0])
    taken.update(now)
    outs, arrived, (part,) = gather(
        base, local, [sender(b) for b in now], 0, traffic, next(idents), owner_sums(pack, 2 * len(now))
    )
    net.land(plan, arrived)
    slots.append(outs)
    outputs = emit(image_count, middle, sum_own, net.block("M", far), total)
    row_slots = [pair[0] for pair in slots]
    grad_slots = [pair[1] for pair in slots]
    (keep_in, send_in, keep_out, send_out, d_bias, d_out_bias), _, (owned,) = slice_grads(
        row_slots, grad_slots, expert_in, expert_in_bias, expert_out, copy_sums(part, (0, 3, 6, 9, 12, 15)), next(idents)
    )
    owned = owned.reshape(width // 2, -1).astype(F32)
    swap = [(i, i ^ 1) for i in range(16)]
    got_in, got_out, got_bias, got_out_bias = (
        lax.ppermute(v, "rep", swap) for v in (send_in, send_out, d_bias, d_out_bias)
    )
    bias = (d_bias + got_bias)[:, 0]
    out_bias = (d_out_bias + got_out_bias)[:, 0]
    half = bias.shape[1] // 2
    piece = width // 16
    expert_grads = (
        keep_in + got_in.astype(F32),
        lax.dynamic_slice_in_dim(bias, core * half, half, axis=1),
        keep_out + got_out.astype(F32),
        lax.dynamic_slice_in_dim(out_bias, device * piece, piece, axis=1),
    )

    balance_loss = jnp.sum(aux * prob_total)
    lines = jnp.transpose(owned[:, 4 * width + EXPERTS : 4 * width + EXPERTS + 8])
    owned = (
        lines[0],
        lines[1],
        owned[:, : 3 * width],
        lines[2],
        lines[3],
        owned[:, 3 * width : 4 * width],
        lines[4],
        lines[5],
        lines[6],
        owned[:, 4 * width : 4 * width + EXPERTS],
    )
    return (outputs, grad_tokens, balance_loss) + owned + expert_grads


def solution(mesh):
    in_specs = (
        P(("rep", "fsdp"), None),
        P(("rep", "fsdp"), None),
        P(("rep", "fsdp"), None),
        P(("rep", "fsdp")),
        P(("rep", "fsdp")),
        P("fsdp"),
        P("fsdp"),
        P("fsdp", None),
        P("fsdp"),
        P("fsdp"),
        P("fsdp", None),
        P("fsdp"),
        P("fsdp"),
        P("fsdp"),
        P("fsdp", None),
        P("fsdp", None, None),
        P("fsdp", None),
        P("fsdp", None, None),
        P("fsdp", None),
    )
    out_specs = (
        P(("rep", "fsdp"), None),
        P(("rep", "fsdp"), None),
        P(),
        P("fsdp"),
        P("fsdp"),
        P("fsdp", None),
        P("fsdp"),
        P("fsdp"),
        P("fsdp", None),
        P("fsdp"),
        P("fsdp"),
        P("fsdp"),
        P("fsdp", None),
        P("fsdp", None, "rep"),
        P("fsdp", "rep"),
        P("fsdp", "rep", None),
        P("fsdp", "rep"),
    )
    program = by_slice if mesh.shape["rep"] == 16 and mesh.shape["fsdp"] == 2 else shards
    return jax.shard_map(program, mesh=mesh, in_specs=in_specs, out_specs=out_specs, check_vma=False)
```

profile of v0, /device:TPU:0, one launch (start us, length us, event | category | flops | bytes accessed | tf_op | source)
XLA Modules:
  0.0 468.8 jit_solution(843183233537034575)
XLA Ops:
  0.7 0.0 copy-start.2
  2.0 1.7 copy.40.refs_4_
  3.7 0.7 stack.24
  4.4 0.7 stack.25
  5.0 0.7 stack.26
  5.7 0.7 stack.27
  6.3 0.7 stack.28
  7.0 0.7 stack.29
  7.7 0.7 stack.30
  8.3 0.8 copy.39
  9.1 1.6 copy.41.refs_5_.refs_17_
  10.7 1.4 copy.42.refs_7_
  12.1 2.1 fusion.1.refs_5_.refs_4_.refs_16_
  14.2 0.0 copy-done.2
  14.2 0.8 fusion.3.refs_6_.refs_18_
  15.0 21.8 %prepare.1 = (bf16[5,208,512]{2,1,0:T(8,128)(2,1)}, bf16[5,208,512]{2,1,0:T(8,128)(2,1)}, s32[5,208,2]{2,1,0:T(8,128)}, f32[5,8,208]{2,1,0:T(8,128)}, f32[1,8,12...) custom-call(s32[1]{0:T(128)S(6)} %copy.47.refs_0_.refs_3_.count_ref, s32[1]{0:T(128)S(6)} %copy.48.refs_1_, ...), custom_call_target="tpu_custom_call" | custom-call | flops 300000000 | bytes 6000000 | tf_op jit(solution)/shard_map/prepare/pallas_call | solution.py:603
  36.7 29.5 %front.1 = (bf16[5,208,1536]{2,1,0:T(8,128)(2,1)}, bf16[5,8,208,208]{3,2,1,0:T(8,128)(2,1)}, bf16[5,208,512]{2,1,0:T(8,128)(2,1)}, f32[5,208,512]{2,1,0:T(8,128)...) custom-call(s32[1]{0:T(128)S(6)} %copy.47.refs_0_.refs_3_.count_ref,, ...), custom_call_target="tpu_custom_call" | custom-call | flops 6000000000 | bytes 16000000 | tf_op jit(solution)/shard_map/front/pallas_call | solution.py:603
  66.3 34.4 %gather.8 = (bf16[16,1,80,512]{3,2,1,0:T(8,128)(2,1)}, bf16[16,1,80,512]{3,2,1,0:T(8,128)(2,1)}, bf16[1,208,512]{2,1,0:T(8,128)(2,1)}, bf16[1,208,512]{2,1,0:T(8...) custom-call(s32[1]{0:T(128)} %bitcast.refs_0_, ...), custom_call_target="tpu_custom_call" | custom-call | flops 2726297600 | bytes 4751360 | tf_op jit(solution)/shard_map/gather/pallas_call | solution.py:603
  100.7 17.2 %gather.9 = (bf16[16,1,80,512]{3,2,1,0:T(8,128)(2,1)}, bf16[16,1,80,512]{3,2,1,0:T(8,128)(2,1)}, bf16[2,208,512]{2,1,0:T(8,128)(2,1)}, bf16[1,208,512]{2,1,0:T(8...) custom-call(s32[1]{0:T(128)} %bitcast.refs_0_, ...), custom_call_target="tpu_custom_call" | custom-call | flops 2726297600 | bytes 4751360 | tf_op jit(solution)/shard_map/gather/pallas_call | solution.py:603
  117.9 63.7 %expert_layer.1 = (bf16[16,80,512]{2,1,0:T(8,128)(2,1)}, bf16[16,80,512]{2,1,0:T(8,128)(2,1)}, bf16[16,80,512]{2,1,0:T(8,128)(2,1)}, bf16[16,80,512]{2,1,0:T(8,1...) custom-call(bf16[16,1,80,512]{3,2,1,0:T(8,128)(2,1)} %get-tuple-elem, ...), custom_call_target="tpu_custom_call" | custom-call | flops 21474836480 | bytes 67108864 | tf_op jit(solution)/shard_map/expert_layer/pallas_call | solution.py:603
  181.7 0.7 slice_bitcast_fusion.1
  182.3 0.6 slice.51
  183.6 0.7 multiply_divide_fusion
  184.3 1.8 fusion.4
  186.1 12.5 %combine.2 = (bf16[5,208,512]{2,1,0:T(8,128)(2,1)}, bf16[5,208,512]{2,1,0:T(8,128)(2,1)}, f32[5,8,208]{2,1,0:T(8,128)}, bf16[1,208,512]{2,1,0:T(8,128)(2,1)}, bf...) custom-call(s32[1]{0:T(128)} %bitcast.refs_0_, ...), custom_call_target="tpu_custom_call" | custom-call | flops 4089446400 | bytes 6000000 | tf_op jit(solution)/shard_map/combine/pallas_call | solution.py:603
  198.6 12.3 %combine.3 = (bf16[5,208,512]{2,1,0:T(8,128)(2,1)}, bf16[5,208,512]{2,1,0:T(8,128)(2,1)}, f32[5,8,208]{2,1,0:T(8,128)}, bf16[1,208,512]{2,1,0:T(8,128)(2,1)}, bf...) custom-call(s32[1]{0:T(128)} %bitcast.refs_0_, ...), custom_call_target="tpu_custom_call" | custom-call | flops 4089446400 | bytes 6000000 | tf_op jit(solution)/shard_map/combine/pallas_call | solution.py:603
  210.9 18.4 %gather.10 = (bf16[16,2,80,512]{3,2,1,0:T(8,128)(2,1)}, bf16[16,2,80,512]{3,2,1,0:T(8,128)(2,1)}, bf16[2,208,512]{2,1,0:T(8,128)(2,1)}, bf16[3,208,512]{2,1,0:T(...) custom-call(s32[1]{0:T(128)} %bitcast.refs_0_, ...), custom_call_target="tpu_custom_call" | custom-call | flops 5452595200 | bytes 9502720 | tf_op jit(solution)/shard_map/gather/pallas_call | solution.py:603
  229.3 39.3 %finish.1 = (f32[985,512]{1,0:T(8,128)}, bf16[2,2,2,64,2176]{4,3,2,1,0:T(8,128)(2,1)}, bf16[2,208,512]{2,1,0:T(8,128)(2,1)}, bf16[4,208,512]{2,1,0:T(8,128)(2,1)...) custom-call(bf16[2,208,512]{2,1,0:T(8,128)(2,1)} %get-tuple-element., ...), custom_call_target="tpu_custom_call" | custom-call | flops 12000000000 | bytes 24000000 | tf_op jit(solution)/shard_map/finish/pallas_call | solution.py:603
  268.6 29.3 %gather.11 = (bf16[16,3,80,512]{3,2,1,0:T(8,128)(2,1)}, bf16[16,3,80,512]{3,2,1,0:T(8,128)(2,1)}, bf16[1,208,512]{2,1,0:T(8,128)(2,1)}, bf16[1,208,512]{2,1,0:T(...) custom-call(s32[1]{0:T(128)} %bitcast.refs_0_, ...), custom_call_target="tpu_custom_call" | custom-call | flops 8178892800 | bytes 14254080 | tf_op jit(solution)/shard_map/gather/pallas_call | solution.py:603
  298.0 31.1 %gather.12 = (bf16[16,3,80,512]{3,2,1,0:T(8,128)(2,1)}, bf16[16,3,80,512]{3,2,1,0:T(8,128)(2,1)}, bf16[2,208,512]{2,1,0:T(8,128)(2,1)}, bf16[1,208,512]{2,1,0:T(...) custom-call(s32[1]{0:T(128)} %bitcast.refs_0_, ...), custom_call_target="tpu_custom_call" | custom-call | flops 8178892800 | bytes 14254080 | tf_op jit(solution)/shard_map/gather/pallas_call | solution.py:603
  329.1 28.4 %gather.13 = (bf16[16,2,80,512]{3,2,1,0:T(8,128)(2,1)}, bf16[16,2,80,512]{3,2,1,0:T(8,128)(2,1)}, bf16[2,208,512]{2,1,0:T(8,128)(2,1)}, bf16[2,208,512]{2,1,0:T(...) custom-call(s32[1]{0:T(128)} %bitcast.refs_0_, ...), custom_call_target="tpu_custom_call" | custom-call | flops 5452595200 | bytes 9502720 | tf_op jit(solution)/shard_map/gather/pallas_call | solution.py:603
  357.5 19.8 %gather.14 = (bf16[16,2,80,512]{3,2,1,0:T(8,128)(2,1)}, bf16[16,2,80,512]{3,2,1,0:T(8,128)(2,1)}, bf16[3,208,512]{2,1,0:T(8,128)(2,1)}, bf16[3,208,512]{2,1,0:T(8,128)(2,1)}, bf16[1,208,512]{2,1,0:T(8,128)(2,1)}) custom-call(s32[1]{0:T(128)} %bitcast.refs_0_, bf16[1,208,512]{2,1,0:T(8,128)(2,1)} %get-tuple-element.215.refs_24_.refs_1_, ...), custom_call_target="tpu_custom_call" | custom-call | flops 5452595200 | bytes 9502720 | tf_op jit(solution)/shard_map/gather/pallas_call | solution.py:603
  377.3 22.7 %gather.15 = (bf16[16,2,80,512]{3,2,1,0:T(8,128)(2,1)}, bf16[16,2,80,512]{3,2,1,0:T(8,128)(2,1)}, bf16[2,64,2176]{2,1,0:T(8,128)(2,1)}) custom-call(s32[1]{0:T(128)} %bitcast.refs_0_, bf16[3,208,512]{2,1,0:T(8,128)(2,1)} %get-tuple-element.259.refs_1_, bf16[2,208,512]{2,1,0:T(8,128)(2,1)} %get-tuple-element.260.refs_2_, ...), custom_call_target="tpu_custom_call" | custom-call | flops 5452595200 | bytes 9502720 | tf_op jit(solution)/shard_map/gather/pallas_call | solution.py:603
  400.0 45.2 %slice_grads.1 = (f32[16,512,128]{2,1,0:T(8,128)}, bf16[16,512,128]{2,1,0:T(8,128)(2,1)}, f32[16,128,512]{2,1,0:T(8,128)}, bf16[16,128,512]{2,1,0:T(8,128)(2,1)}...) custom-call(bf16[16,1,80,512]{3,2,1,0:T(8,128)(2,1)} %get-tuple-element.161.refs_0_, ...), custom_call_target="tpu_custom_call" | custom-call | flops 21474836480 | bytes 67108864 | tf_op jit(solution)/shard_map/slice_grads/pallas_call | solution.py:603
  445.3 0.1 collective-permute-start
  445.3 0.5 collective-permute-start.2
  445.8 0.1 collective-permute-start.1
  445.9 0.4 collective-permute-start.3
  446.3 1.4 bitcast_convert_fusion
  447.7 0.1 slice_bitcast_fusion
  447.8 1.1 slice_reduce_fusion
  449.0 1.3 slice.67
  450.3 0.9 slice.70
  451.2 0.7 copy.45
  451.9 0.0 copy-start.3
  451.9 5.1 %emit.1 = bf16[985,512]{1,0:T(8,128)(2,1)} custom-call(s32[1]{0:T(128)S(6)} %copy.47.refs_0_.refs_3_.count_ref, f32[5,208,512]{2,1,0:T(8,128)} %get-tuple-element.157.refs_9_.middle_ref, bf16[5,208,512]{2,1,0:T(8,128)(2,1)} %get-tuple-element.185.own_ref, bf16[2,208,512]{2,1,0:T(8,128)(2,1)} %get-tuple-element.243.refs_0_, ...), custom_call_target="tpu_custom_call" | custom-call | flops 2000000 | bytes 6000000 | tf_op jit(solution)/shard_map/emit/pallas_call | solution.py:558
  457.0 0.0 collective-permute-done.1
  457.0 0.0 copy-done.3
  457.0 0.6 dynamic-slice_add_fusion.1
  457.6 0.0 collective-permute-done.3
  457.6 1.4 dynamic-slice_add_fusion
  459.0 0.0 collective-permute-done
  459.0 0.0 copy-start
  459.0 5.4 %convert_add_fusion.1 = f32[16,512,128]{2,1,0:T(8,128)} fusion(f32[16,512,128]{2,1,0:T(8,128)} %get-tuple-element.279, bf16[16,512,128]{2,1,0:T(8,128)(2,1)} %collective-permute-done), kind=kLoop, calls=%fused_computation.1 | loop fusion | flops 2097152 | bytes 10485760 | tf_op jit(solution)/shard_map/add | solution.py:1731
  464.4 0.0 collective-permute-done.2
  464.4 0.0 copy-done
  464.4 0.0 copy-start.1
  464.4 2.8 convert_add_fusion
  467.3 0.0 copy-done.1
  467.3 1.3 copy.49
  (2 shorter events, 0.0 us)
Async XLA Ops:
  0.7 13.6 %copy-start.2 = (bf16[256,512]{1,0:T(8,128)(2,1)S(1)}, bf16[256,512]{1,0:T(8,128)(2,1)}, u32[]{:S(2)}) copy-start(bf16[256,512]{1,0:T(8,128)(2,1)} %param.29) | copy-start | bytes 786436
  445.3 13.7 %collective-permute-start = (bf16[16,512,128]{2,1,0:T(8,128)(2,1)}, bf16[16,512,128]{2,1,0:T(8,128)(2,1)}, u32[]{:S(2)}, u32[]{:S(2)}) collective-permute-start(bf16[16,512,128]{2,1,0:T(8,128)(2,1)} %get-tuple-element.280), channel_id=1, source_target_pairs={{0,2},{2,0},{4,6},{6,4},{8,10},{10,8},{12,14},{14,12},{16,18},{18,... | collective-permute-start | bytes 6291464 | tf_op jit(solution)/shard_map/ppermute | solution.py:1724
  445.3 19.1 %collective-permute-start.2 = (bf16[16,128,512]{2,1,0:T(8,128)(2,1)}, bf16[16,128,512]{2,1,0:T(8,128)(2,1)S(1)}, u32[]{:S(2)}, u32[]{:S(2)}) collective-permute-start(bf16[16,128,512]{2,1,0:T(8,128)(2,1)} %get-tuple-element.283), channel_id=1, source_target_pairs={{0,2},{2,0},{4,6},{6,4},{8,10},{10,8},{12,14},{14,12},{16,18},{18,... | collective-permute-start | bytes 6291464 | tf_op jit(solution)/shard_map/ppermute | solution.py:1724
  445.8 11.1 %collective-permute-start.1 = (f32[16,1,256]{2,1,0:T(1,128)}, f32[16,1,256]{2,1,0:T(1,128)S(1)}, u32[]{:S(2)}, u32[]{:S(2)}) collective-permute-start(f32[16,1,256]{2,1,0:T(1,128)} %get-tuple-element.281), channel_id=1, source_target_pairs={{0,2},{2,0},{4,6},{6,4},{8,10},{10,8},{12,14},{14,12},{16,18},{18,... | collective-permute-start | bytes 49160 | tf_op jit(solution)/shard_map/ppermute | solution.py:1724
  445.9 11.7 %collective-permute-start.3 = (f32[16,1,512]{2,1,0:T(1,128)}, f32[16,1,512]{2,1,0:T(1,128)S(1)}, u32[]{:S(2)}, u32[]{:S(2)}) collective-permute-start(f32[16,1,512]{2,1,0:T(1,128)} %get-tuple-element.284), channel_id=1, source_target_pairs={{0,2},{2,0},{4,6},{6,4},{8,10},{10,8},{12,14},{14,12},{16,18},{18,... | collective-permute-start | bytes 98312 | tf_op jit(solution)/shard_map/ppermute | solution.py:1724
  451.9 5.1 %copy-start.3 = (f32[16,1,256]{2,1,0:T(1,128)S(1)}, f32[16,1,256]{2,1,0:T(1,128)}, u32[]{:S(2)}) copy-start(f32[16,1,256]{2,1,0:T(1,128)} %get-tuple-element.281) | copy-start | bytes 49156
  459.0 5.4 %copy-start = (f32[16,128,512]{2,1,0:T(8,128)S(1)}, f32[16,128,512]{2,1,0:T(8,128)}, u32[]{:S(2)}) copy-start(f32[16,128,512]{2,1,0:T(8,128)} %get-tuple-element.282) | copy-start | bytes 12582916
  464.4 2.8 copy-start.1
where the time goes:
time: 478 us; the launch traced here: 469 us
  Pallas kernels  431 us (90%)
  other arithmetic  17 us (4%)
  local copies, waits for them, and re-layouts  16.8 us (4%)
    pallas_call x15, Pallas kernels, run(): pl.pallas_call(carried, grid=grid, in_specs=list(in_specs) + [anywhere] *...  426 us
  transfers between devices with their start and end apart: 4, of which 0 were waited for; matrix products, arithmetic and copies ran while one was open for 3% of the time, Pallas kernels for 1%

commit v1 on v0

--- a/solution.py
+++ b/solution.py
@@ -505,6 +505,13 @@
                     only_if(moves[index].roles()[1], moves[index].copy(refs, send.at[index], recv.at[index]).wait_recv)
             only_if(move.roles()[0], move.copy(refs, send.at[at + k], recv.at[at + k]).start)
 
+    def require(self, target, position, refs, send, recv, arrived):
+        moves = [m for moves in self.rounds for m in moves]
+        for index, move in enumerate(moves):
+            if move.home[0] == target and move.home[1] <= position < move.home[1] + move.size and index not in arrived:
+                arrived.add(index)
+                only_if(move.roles()[1], move.copy(refs, send.at[index], recv.at[index]).wait_recv)
+
     def finish(self, refs, send, recv, arrived):
         moves = [m for moves in self.rounds for m in moves]
         for index, move in enumerate(moves):
@@ -552,7 +559,7 @@
 
 def run(
     body, args, in_specs, out_specs, out_shape, *,
-    name, grid=(1,), scratch=(), cost=None, traffic=None, chain=None, ident=None,
+    name, grid=(1,), scratch=(), cost=None, traffic=None, chain=None, hook=None, ident=None,
 ):
     if (traffic is None or traffic.count() == 0) and chain is None:
         outs = pl.pallas_call(
@@ -577,17 +584,23 @@
         step = pl.program_id(0)
         pl.when(step == 0)(lambda: greet(links))
         arrived = set()
-        for which, at in enumerate(traffic.steps):
-
-            @pl.when(step == at)
-            def _():
-                traffic.start(which, ends, *refs, arrived)
-
-        for at, action in chain.actions[:-1]:
-
-            @pl.when(step == at)
-            def _():
-                action(*chain_in, *chain_out, *chain_held)
+        for at in range(grid[0]):
+            rounds = [which for which, when in enumerate(traffic.steps) if when == at]
+            actions = [action for when, action in chain.actions[:-1] if when == at]
+            if rounds or actions or hook:
+
+                @pl.when(step == at)
+                def _():
+                    for which in rounds:
+                        traffic.start(which, ends, *refs, arrived)
+                    for action in actions:
+                        action(*chain_in, *chain_out, *chain_held)
+                    if hook:
+                        hook(
+                            at,
+                            lambda target, position: traffic.require(target, position, ends, *refs, arrived),
+                            targets, ins, held,
+                        )
 
         body(*ins, *outs, *held)
 
@@ -616,40 +629,41 @@
 
 COT_PATHS = {
     (0, 0, 1): ("y", (0, 0, 0), -1.500),
-    (0, 1, 0): ("x", (0, 0, 0), 3.002),
-    (0, 1, 1): ("x", (0, 0, 1), 2.463),
-    (1, 0, 0): ("near", (0, 0, 0), 5.503),
-    (1, 0, 1): ("y", (1, 0, 0), 0.791),
-    (1, 1, 0): ("near", (0, 1, 0), 0.934),
-    (1, 1, 1): ("x", (1, 0, 1), 1.171),
-    (2, 0, 0): ("reach", (0, 0, 0), 2.419),
-    (2, 0, 1): ("y", (2, 0, 0), 2.680),
-    (2, 1, 0): ("reach", (0, 1, 0), 0.624),
-    (2, 1, 1): ("x", (2, 0, 1), 5.712),
-    (3, 0, 0): ("inner", (1, 0, 0), 0.725),
-    (3, 0, 1): ("y", (3, 0, 0), 2.905),
-    (3, 1, 0): ("x", (3, 0, 0), 4.267),
-    (3, 1, 1): ("x", (3, 0, 1), 3.366),
+    (0, 1, 0): ("x", (0, 0, 0), 2.243),
+    (0, 1, 1): ("x", (0, 0, 1), 1.258),
+    (1, 0, 0): ("near", (0, 0, 0), 1.763),
+    (1, 0, 1): ("near", (0, 0, 1), 1.701),
+    (1, 1, 0): ("near", (0, 1, 0), 3.477),
+    (1, 1, 1): ("x", (1, 0, 1), 5.719),
+    (2, 0, 0): ("inner", (0, 0, 0), 4.656),
+    (2, 0, 1): ("y", (2, 0, 0), 2.464),
+    (2, 1, 0): ("inner", (0, 1, 0), 0.237),
+    (2, 1, 1): ("x", (2, 0, 1), 2.798),
+    (3, 0, 0): ("inner", (1, 0, 0), 0.958),
+    (3, 0, 1): ("y", (3, 0, 0), 2.984),
+    (3, 1, 0): ("x", (3, 0, 0), 2.092),
+    (3, 1, 1): ("inner", (1, 1, 1), 1.507),
 }
 ROW_PATHS = {
     (0, 0, 1): ("y", (0, 0, 0), -1.400),
-    (0, 1, 0): ("x", (0, 0, 0), 0.507),
-    (0, 1, 1): ("x", (0, 0, 1), 3.006),
-    (1, 0, 0): ("near", (0, 0, 0), 4.270),
-    (1, 0, 1): ("y", (1, 0, 0), 1.765),
-    (1, 1, 0): ("near", (0, 1, 0), 5.532),
-    (1, 1, 1): ("x", (1, 0, 1), 0.781),
-    (2, 0, 0): ("inner", (0, 0, 0), 2.116),
-    (2, 0, 1): ("y", (2, 0, 0), 1.823),
-    (2, 1, 0): ("x", (2, 0, 0), 0.695),
-    (2, 1, 1): ("y", (2, 1, 0), 3.141),
-    (3, 0, 0): ("reach", (1, 0, 0), 3.737),
-    (3, 0, 1): ("y", (3, 0, 0), 2.332),
-    (3, 1, 0): ("inner", (1, 1, 0), 3.735),
-    (3, 1, 1): ("x", (3, 0, 1), 4.908),
+    (0, 1, 0): ("x", (0, 0, 0), 1.939),
+    (0, 1, 1): ("x", (0, 0, 1), 1.580),
+    (1, 0, 0): ("near", (0, 0, 0), 1.441),
+    (1, 0, 1): ("y", (1, 0, 0), 0.198),
+    (1, 1, 0): ("near", (0, 1, 0), 2.429),
+    (1, 1, 1): ("x", (1, 0, 1), 5.646),
+    (2, 0, 0): ("inner", (0, 0, 0), 2.268),
+    (2, 0, 1): ("y", (2, 0, 0), 2.650),
+    (2, 1, 0): ("x", (2, 0, 0), 4.955),
+    (2, 1, 1): ("x", (2, 0, 1), 4.985),
+    (3, 0, 0): ("reach", (1, 0, 0), 1.374),
+    (3, 0, 1): ("y", (3, 0, 0), 4.956),
+    (3, 1, 0): ("x", (3, 0, 0), 2.903),
+    (3, 1, 1): ("y", (3, 1, 0), 4.968),
 }
 FAR_FIRST = {(0, 0, 1): ("y", (0, 0, 0), -2.0)}
-FAR_LAST = {(0, 0, 1): ("y", (0, 0, 0), 5.198)}
+FAR_LAST = {(0, 0, 1): ("y", (0, 0, 0), 2.506)}
+FRONT_ROOM, PAIR_ROOM, EXPERT_ROOM, OWN_ROOM, FINISH_ROOM, LAST_ROOM = 5, 9, 11, 4, 8, 25
 
 
 class Network:
@@ -774,7 +788,21 @@
         while moves and not moves[-1]:
             moves.pop()
         traffic = Traffic(sources, targets, moves, steps[: len(moves)])
-        return traffic, (order, homes)
+        return traffic, (order, homes, landed)
+
+    def find(self, plan, name, block):
+        order, homes, landed = plan
+        found = []
+        for p in range(self.pieces[name]):
+            if (name, block, p) in landed:
+                found.append((None, order.index((name, block)), homes[name, block].index(p)))
+            else:
+                array, at = self.have[name, block, p]
+                found.append((array, None, at))
+        return found
+
+    def landing(self, plan, block):
+        return max(plan[2].get((name, block, p), 0.0) for name in "CS" for p in range(self.pieces[name]))
 
     @staticmethod
     def move(link, origin, home, count, needs):
@@ -789,7 +817,7 @@
         return made
 
     def land(self, plan, arrays):
-        order, homes = plan
+        order, homes, _ = plan
         for key, array in zip(order, arrays):
             for at, p in enumerate(homes[key]):
                 self.have[key[0], key[1], p] = (array, at)
@@ -1034,76 +1062,117 @@
     return meta[0:1] * CAP + meta[1:2], meta[2:3] * CAP + meta[3:4]
 
 
-def gather_body(base_ref, *refs, parts, senders):
-    arrays, (row_out, grad_out, rows, lines) = refs[:parts], refs[parts:]
-    experts, _, cap, width = row_out.shape
-    slots = experts * cap
-    tokens = rows.shape[0]
-    step = pl.program_id(0)
-    for k, pair in enumerate(senders):
-        for kind, pieces in enumerate(pair):
-
-            @pl.when(step == 2 * k + kind)
+def gather(base, experts, senders, sequence, traffic, ident, chain=None):
+    arrays, table = [], []
+    for sender in sequence:
+        if sender is None:
+            table.append(None)
+            continue
+        for kind in range(2):
+            spots = []
+            for array, target, position in senders[sender][kind]:
+                at = target
+                if array is not None:
+                    at = next((k for k, known in enumerate(arrays) if known is array), len(arrays))
+                    if at == len(arrays):
+                        arrays.append(array)
+                spots.append((array is None, at, position))
+            table.append((sender, kind, spots))
+    images, width = len(table[0][2]), arrays[0].shape[-1]
+    tokens, slots, count, steps = images * PAD, experts * CAP, len(senders), len(table)
+    first = [next(k for k, entry in enumerate(table) if entry and entry[0] == sender) for sender in range(count)]
+
+    def hook(step, require, targets, ins, held):
+        sources, rows, loaded = ins[1:], held[0], held[2]
+
+        def copies(entry):
+            _, kind, spots = entry
+            return [
+                pltpu.make_async_copy(
+                    (targets if arriving else sources)[at].at[position],
+                    rows.at[kind, pl.ds(image * PAD, PAD)],
+                    loaded.at[kind, image],
+                )
+                for image, (arriving, at, position) in enumerate(spots)
+            ]
+
+        def load(entry):
+            for arriving, at, position in entry[2]:
+                if arriving:
+                    require(at, position)
+            for copy in copies(entry):
+                copy.start()
+
+        if step == 0:
+            load(table[0])
+        if step + 1 < steps and table[step + 1]:
+            load(table[step + 1])
+        if table[step]:
+            for copy in copies(table[step]):
+                copy.wait()
+
+    def body(base_ref, *refs):
+        row_out, grad_out, rows, lines = refs[len(arrays) : len(arrays) + 4]
+        step = pl.program_id(0)
+        turns = [(k, entry[1]) for k, entry in enumerate(table) if entry]
+        working, gated = step < 0, step < 0
+        for k, kind in turns:
+            working = working | (step == k)
+            if kind:
+                gated = gated | (step == k)
+
+        @pl.when(working & ~gated)
+        def _():
+            for image in range(images):
+                lines[image] = rows[0, image * PAD + PAD - 16 : (image + 1) * PAD, :PAD].astype(F32)[8:]
+
+        @pl.when(working)
+        def _():
+            meta = jnp.concatenate([lines[image] for image in range(images)], axis=1)
+            one, two = slot_lines(meta)
+            weight_one = jnp.where(gated, meta[4:5], 1.0)
+            weight_two = jnp.where(gated, meta[5:6], 1.0)
+            slot = (iota((slots, tokens), 0) + base_ref[0]).astype(F32)
+            pick = jnp.where(slot == one, weight_one, 0.0) + jnp.where(slot == two, weight_two, 0.0)
+            got = dot(pick.astype(BF16), rows[jnp.where(gated, 1, 0)])
+            got = got.astype(BF16).reshape(experts, 1, CAP, width)
+
+            @pl.when(~gated)
             def _():
-                for image, (at, position) in enumerate(pieces):
-                    value = arrays[at][position]
-                    rows[image * PAD : (image + 1) * PAD, :] = value
-                    if kind == 0:
-                        lines[image] = value[PAD - 16 :, :PAD].astype(F32)[8:]
-
-    @pl.when(step < 2 * len(senders))
-    def _():
-        meta = jnp.concatenate([lines[image] for image in range(lines.shape[0])], axis=1)
-        one, two = slot_lines(meta)
-        gated = step % 2 == 1
-        weight_one = jnp.where(gated, meta[4:5], 1.0)
-        weight_two = jnp.where(gated, meta[5:6], 1.0)
-        slot = (iota((slots, tokens), 0) + base_ref[0]).astype(F32)
-        pick = jnp.where(slot == one, weight_one, 0.0) + jnp.where(slot == two, weight_two, 0.0)
-        got = dot(pick.astype(BF16), rows[...]).astype(BF16).reshape(experts, 1, cap, width)
-
-        @pl.when(step % 2 == 0)
-        def _():
-            row_out[...] = got
-
-        @pl.when(step % 2 == 1)
-        def _():
-            grad_out[...] = got
-
-
-def gather(base, experts, senders, extra, traffic, ident, chain=None):
-    arrays, table = [], []
-    for pair in senders:
-        table.append([])
-        for pieces in pair:
-            table[-1].append([])
-            for array, position in pieces:
-                at = next((k for k, known in enumerate(arrays) if known is array), len(arrays))
-                if at == len(arrays):
-                    arrays.append(array)
-                table[-1][-1].append((at, position))
-    width = arrays[0].shape[-1]
-    images = len(table[0][0])
-    tokens = images * PAD
-    count = len(senders)
+                row_out[...] = got
+
+            @pl.when(gated)
+            def _():
+                grad_out[...] = got
+
+    def place(d):
+        turn = 0
+        for at in first[1:]:
+            turn += jnp.where(d >= at, 1, 0)
+        return (0, turn, 0, 0)
+
     shape = jax.ShapeDtypeStruct((experts, count, CAP, width), BF16)
     return run(
-        lambda *refs: gather_body(*refs, parts=len(arrays), senders=table),
+        body,
         (base, *arrays),
-        [scalar_spec()]
-        + [pl.BlockSpec(a.shape, lambda d: (0, 0, 0), pipeline_mode=pl.Buffered(1)) for a in arrays],
-        [pl.BlockSpec((experts, 1, CAP, width), lambda d: (0, jnp.minimum(d // 2, count - 1), 0, 0))] * 2,
+        [scalar_spec()] + [pl.BlockSpec(memory_space=pl.ANY)] * len(arrays),
+        [pl.BlockSpec((experts, 1, CAP, width), place)] * 2,
         [shape, shape],
-        grid=(2 * count + extra,),
-        scratch=[pltpu.VMEM((tokens, width), BF16), pltpu.VMEM((images, 8, PAD), F32)],
+        grid=(steps,),
+        scratch=[
+            pltpu.VMEM((2, tokens, width), BF16),
+            pltpu.VMEM((images, 8, PAD), F32),
+            pltpu.SemaphoreType.DMA((2, images)),
+        ],
         cost=pl.CostEstimate(
-            flops=4 * count * experts * CAP * tokens * width,
-            bytes_accessed=4 * count * (tokens + experts * CAP) * width,
+            flops=4 * count * slots * tokens * width,
+            bytes_accessed=4 * count * (tokens + slots) * width,
             transcendentals=0,
         ),
         name="gather",
         traffic=traffic,
         chain=chain,
+        hook=hook,
         ident=ident,
     )
 
@@ -1130,24 +1199,24 @@
     back_own[0], back_far[0] = back[:cap], back[cap:]
 
 
-def expert_layer(own, far, first, first_bias, second, second_bias, chain, traffic, ident):
-    experts, _, cap, width = own[0].shape
+def expert_layer(pair, first, first_bias, second, second_bias, chain, traffic, ident):
+    experts, _, cap, width = pair[0].shape
     hidden = first.shape[2]
-    rows = pl.BlockSpec((1, 1, cap, width), lambda e: (e, 0, 0, 0))
+    rows = [pl.BlockSpec((1, 1, cap, width), lambda e, side=side: (e, side, 0, 0)) for side in range(2)]
     out = pl.BlockSpec((1, cap, width), lambda e: (e, 0, 0))
     return run(
         expert_body,
         (
-            own[0],
-            far[0],
-            own[1],
-            far[1],
+            pair[0],
+            pair[0],
+            pair[1],
+            pair[1],
             first,
             first_bias.reshape(experts, 1, hidden),
             second,
             second_bias.reshape(experts, 1, width),
         ),
-        [rows] * 4 + [by_image(width, hidden), by_image(1, hidden), by_image(hidden, width), by_image(1, width)],
+        rows + rows + [by_image(width, hidden), by_image(1, hidden), by_image(hidden, width), by_image(1, width)],
         [out] * 4,
         [jax.ShapeDtypeStruct((experts, cap, width), BF16)] * 4,
         grid=(experts,),
@@ -1355,14 +1424,28 @@
     packed, prob, mixed, middle, second, soft = saved
     shape = jax.ShapeDtypeStruct
     tile = by_image(PAD, width)
-    row_arrays, row_specs, read_rows = by_piece(row_far, PAD, width)
+    row_arrays = []
+    for array, _, _ in row_far:
+        if array is not None and not any(known is array for known in row_arrays):
+            row_arrays.append(array)
     gate_arrays, gate_specs, read_gates = by_piece(gate_far, 8, PAD)
-    extra = len(row_arrays) + len(gate_arrays)
+    lead, extra = len(row_arrays), len(row_arrays) + len(gate_arrays)
+
+    def hook(step, require, targets, ins, held):
+        array, target, position = row_far[step]
+        if array is None:
+            require(target, position)
+            source = targets[target]
+        else:
+            source = next(ref for ref, known in zip(ins, row_arrays) if known is array)
+        copy = pltpu.make_async_copy(source.at[position], held[-2], held[-1])
+        copy.start()
+        copy.wait()
 
     def body(*refs):
-        pieces, refs = refs[:extra], list(refs[extra:])
-        refs[11:11] = [read_rows(pieces[: len(row_arrays)])]
-        refs[13:13] = [read_gates(pieces[len(row_arrays) :])]
+        pieces, far, refs = refs[:extra], refs[-2], list(refs[extra:-2])
+        refs[11:11] = [far[...]]
+        refs[13:13] = [read_gates(pieces[lead:])]
         finish_body(*refs)
 
     pack = (2, 2, 2, width // 8, 4 * width + 128)
@@ -1373,7 +1456,7 @@
             row_own, gate_own, aux, *wide, *tall,
         ),
         [
-            *row_specs,
+            *[pl.BlockSpec(memory_space=pl.ANY)] * lead,
             *gate_specs,
             scalar_spec(),
             tile,
@@ -1404,10 +1487,13 @@
             pltpu.VMEM((width, width), F32),
             pltpu.VMEM((width, 128), F32),
             pltpu.VMEM((128, width), F32),
+            pltpu.VMEM((PAD, width), BF16),
+            pltpu.SemaphoreType.DMA,
         ],
         cost=pl.CostEstimate(flops=12_000_000_000, bytes_accessed=24_000_000, transcendentals=0),
         name="finish",
         traffic=traffic,
+        hook=hook,
         ident=ident,
     )
 
@@ -1509,7 +1595,7 @@
         [pltpu.VMEM((2,) + shape, BF16), pltpu.VMEM((2,) + shape, BF16), pltpu.VMEM(shape, BF16)]
         + [pltpu.SemaphoreType.DMA((2,))] * 2,
         {"core", "y"},
-        [(0, first), (1, second), (steps, last)],
+        [(steps[0], first), (steps[1], second), (0, last)],
     )
 
 
@@ -1647,39 +1733,31 @@
 
     def staged(kernel, *args, rounds):
         traffic, plan = net.plan(*rounds)
+        args = [arg(plan) if callable(arg) else arg for arg in args]
         outs, arrived, chained = kernel(*args, traffic, next(idents))
         net.land(plan, arrived)
         return (*outs, *chained)
 
     own, far = (0, 0, 0), (0, 0, 1)
     packed, prob, mixed, middle, second, soft, soft_sum = staged(
-        front, image_count, tok, ids, route, wide, tall, rounds=evenly(4, 5, 0.68)
+        front, image_count, tok, ids, route, wide, tall, rounds=evenly(FRONT_ROOM, 5, 0.68)
     )
     net.offer("S", second, ROW_PATHS)
 
     def sender(block):
         return net.block("S", block), net.block("C", block)
 
-    slots = []
-    taken = set()
-
-    def take(blocks, room, extra):
-        taken.update(blocks)
-        outs = staged(
-            gather, base, local, [sender(b) for b in blocks], extra, rounds=gathering(room, len(blocks), extra)
-        )
-        slots.append(outs)
-        return outs
-
-    def ready():
-        return [b for b in COT_PATHS if b not in taken and net.complete("S", b) and net.complete("C", b)]
-
-    slots_own = take([own], 6, 4)
-    slots_far = take([far], 2, 1)
+    def senders(blocks):
+        return lambda plan: [(net.find(plan, "S", block), net.find(plan, "C", block)) for block in blocks]
+
+    pair = staged(
+        gather, base, local, senders([own, far]), [0, None, None, None, None, 1],
+        rounds=(PAIR_ROOM, list(range(8)), [0.0, 0.45, 0.9, 1.9, 2.9, 3.9, 5.0, 6.0]),
+    )
     made_own, made_far, back_own, back_far, sums = staged(
-        expert_layer, slots_own, slots_far, expert_in, expert_in_bias, expert_out, expert_out_bias,
+        expert_layer, pair, expert_in, expert_in_bias, expert_out, expert_out_bias,
         sums_everywhere(load, soft_sum, (0, 2, 5, 8, 11, 13)),
-        rounds=evenly(11, 16, 0.7, 2),
+        rounds=evenly(EXPERT_ROOM, 16, 0.7, 2),
     )
     sum_far, drow_far, dgate_far = staged(
         combine, base, *sender(far), made_far, back_far, rounds=evenly(2, 5, 0.4, 2)
@@ -1688,30 +1766,27 @@
     net.offer("G", dgate_far, FAR_FIRST, 0)
     net.offer("M", sum_far, FAR_LAST)
     sum_own, drow_own, dgate_own = staged(
-        combine, base, *sender(own), made_own, back_own, rounds=evenly(2, 5, 0.4, 2)
-    )
-    take(ready()[:2], 3, 1)
+        combine, base, *sender(own), made_own, back_own, rounds=evenly(OWN_ROOM, 5, 0.4)
+    )
     loads, prob_total = sums[0, 0:1], sums[1, 0:1]
     live = loads[:, 64:65]
     share = (loads[:, :EXPERTS] + loads[:, EXPERTS : 2 * EXPERTS]) / (2.0 * live)
     aux = jnp.pad(EXPERTS * share / live, ((0, 0), (0, 128 - EXPERTS)))
     grad_tokens, pack = staged(
         finish, image_count, tok, cot, (packed, prob, mixed, middle, second, soft), route, drow_own,
-        net.block("D", far), dgate_own, net.block("G", far), aux, wide, tall, total,
-        rounds=evenly(7, 5, 1.5),
-    )
-    while True:
-        now = ready()[:3]
-        if not net.missing() and len(taken) + len(now) == 16:
-            break
-        take(now, 5, 2)
-    traffic, plan = net.plan(0, [0], [0.0])
-    taken.update(now)
+        lambda plan: net.find(plan, "D", far), dgate_own, net.block("G", far), aux, wide, tall, total,
+        rounds=evenly(FINISH_ROOM, 5, 1.5),
+    )
+    blocks = [block for block in COT_PATHS if block != far]
+    count = 2 * len(blocks) + 2
+    traffic, plan = net.plan(LAST_ROOM, list(range(count)), [LAST_ROOM * k / count for k in range(count)])
+    blocks.sort(key=lambda block: net.landing(plan, block))
     outs, arrived, (part,) = gather(
-        base, local, [sender(b) for b in now], 0, traffic, next(idents), owner_sums(pack, 2 * len(now))
+        base, local, senders(blocks)(plan), list(range(len(blocks))) + [None, None],
+        traffic, next(idents), owner_sums(pack, (0, 6)),
     )
     net.land(plan, arrived)
-    slots.append(outs)
+    slots = [pair, outs]
     outputs = emit(image_count, middle, sum_own, net.block("M", far), total)
     row_slots = [pair[0] for pair in slots]
     grad_slots = [pair[1] for pair in slots]

time: 478 us -> 430 us (0.90); the launches traced: 469 us -> 429 us
  Pallas kernels: 431 us -> 391 us
    pallas_call x15 -> x9, Pallas kernels: 426 us -> 386 us  [run(): pl.pallas_call(carried, grid=grid, in_specs=list(in_specs) + [anywhere] *...]
where the time goes in v1:
time: 430 us; the launch traced here: 429 us
  Pallas kernels  391 us (91%)
  other arithmetic  17 us (4%)
  local copies, waits for them, and re-layouts  16.8 us (4%)
    pallas_call x9, Pallas kernels, run(): pl.pallas_call(carried, grid=grid, in_specs=list(in_specs) + [anywhere] *...  386 us
  transfers between devices with their start and end apart: 4, of which 0 were waited for; matrix products, arithmetic and copies ran while one was open for 3% of the time, Pallas kernels for 1%

profile of v1, /device:TPU:0, one launch (start us, length us, event | category | flops | bytes accessed | tf_op | source)
XLA Modules:
  0.0 428.7 jit_solution(14950818960534841099)
XLA Ops:
  0.7 0.0 copy-start.2
  2.0 1.7 copy.40.refs_4_
  3.7 0.7 stack.24
  4.4 0.7 stack.25
  5.0 0.7 stack.26
  5.7 0.7 stack.27
  6.3 0.7 stack.28
  7.0 0.7 stack.29
  7.7 0.7 stack.30
  8.3 0.8 copy.39
  9.1 1.6 copy.41.refs_5_
  10.7 1.4 copy.42.refs_7_
  12.1 2.1 fusion.1.refs_5_.refs_4_.refs_15_
  14.2 0.0 copy-done.2
  14.2 0.8 fusion.3.refs_6_.refs_17_
  15.0 21.7 %prepare.1 = (bf16[5,208,512]{2,1,0:T(8,128)(2,1)}, bf16[5,208,512]{2,1,0:T(8,128)(2,1)}, s32[5,208,2]{2,1,0:T(8,128)}, f32[5,8,208]{2,1,0:T(8,128)}, f32[1,8,12...) custom-call(s32[1]{0:T(128)S(6)} %copy.47.refs_0_.refs_2_.count_ref, s32[1]{0:T(128)S(6)} %copy.48.refs_1_, ...), custom_call_target="tpu_custom_call" | custom-call | flops 300000000 | bytes 6000000 | tf_op jit(solution)/shard_map/prepare/pallas_call | solution.py:616
  36.7 30.8 %front.1 = (bf16[5,208,1536]{2,1,0:T(8,128)(2,1)}, bf16[5,8,208,208]{3,2,1,0:T(8,128)(2,1)}, bf16[5,208,512]{2,1,0:T(8,128)(2,1)}, f32[5,208,512]{2,1,0:T(8,128)...) custom-call(s32[1]{0:T(128)S(6)} %copy.47.refs_0_.refs_2_.count_ref,, ...), custom_call_target="tpu_custom_call" | custom-call | flops 6000000000 | bytes 16000000 | tf_op jit(solution)/shard_map/front/pallas_call | solution.py:616
  67.5 47.5 %gather.2 = (bf16[16,2,80,512]{3,2,1,0:T(8,128)(2,1)}, bf16[16,2,80,512]{3,2,1,0:T(8,128)(2,1)}, bf16[3,208,512]{2,1,0:T(8,128)(2,1)}, bf16[1,208,512]{2,1,0:T(8...) custom-call(s32[1]{0:T(128)} %bitcast.refs_0_, ...), custom_call_target="tpu_custom_call" | custom-call | flops 5452595200 | bytes 9502720 | tf_op jit(solution)/shard_map/gather/pallas_call | solution.py:616
  115.0 61.3 %expert_layer.1 = (bf16[16,80,512]{2,1,0:T(8,128)(2,1)}, bf16[16,80,512]{2,1,0:T(8,128)(2,1)}, bf16[16,80,512]{2,1,0:T(8,128)(2,1)}, bf16[16,80,512]{2,1,0:T(8,1...) custom-call(bf16[16,2,80,512]{3,2,1,0:T(8,128)(2,1)} %get-tuple-elem, ...), custom_call_target="tpu_custom_call" | custom-call | flops 21474836480 | bytes 67108864 | tf_op jit(solution)/shard_map/expert_layer/pallas_call | solution.py:616
  176.3 0.7 slice_bitcast_fusion.1
  176.9 0.6 slice.51
  178.2 0.7 multiply_divide_fusion
  178.9 1.8 fusion.4
  180.7 12.4 %combine.2 = (bf16[5,208,512]{2,1,0:T(8,128)(2,1)}, bf16[5,208,512]{2,1,0:T(8,128)(2,1)}, f32[5,8,208]{2,1,0:T(8,128)}, bf16[1,208,512]{2,1,0:T(8,128)(2,1)}, bf...) custom-call(s32[1]{0:T(128)} %bitcast.refs_0_, bf16[16,80,512]{2,1,0:T(8,128)(2,1)} %get-tuple-element.128.refs_1_, ...), custom_call_target="tpu_custom_call" | custom-call | flops 4089446400 | bytes 6000000 | tf_op jit(solution)/shard_map/combine/pallas_call | solution.py:616
  193.1 21.9 %combine.3 = (bf16[5,208,512]{2,1,0:T(8,128)(2,1)}, bf16[5,208,512]{2,1,0:T(8,128)(2,1)}, f32[5,8,208]{2,1,0:T(8,128)}, bf16[1,208,512]{2,1,0:T(8,128)(2,1)}, bf...) custom-call(s32[1]{0:T(128)} %bitcast.refs_0_, ...), custom_call_target="tpu_custom_call" | custom-call | flops 4089446400 | bytes 6000000 | tf_op jit(solution)/shard_map/combine/pallas_call | solution.py:616
  215.0 42.8 %finish.1 = (f32[985,512]{1,0:T(8,128)}, bf16[2,2,2,64,2176]{4,3,2,1,0:T(8,128)(2,1)}, bf16[1,208,512]{2,1,0:T(8,128)(2,1)}, bf16[3,208,512]{2,1,0:T(8,128)(2,1)...) custom-call(bf16[4,208,512]{2,1,0:T(8,128)(2,1)} %get-tuple-element., ...), custom_call_target="tpu_custom_call" | custom-call | flops 12000000000 | bytes 24000000 | tf_op jit(solution)/shard_map/finish/pallas_call | solution.py:616
  257.8 103.7 %gather.3 = (bf16[16,14,80,512]{3,2,1,0:T(8,128)(2,1)}, bf16[16,14,80,512]{3,2,1,0:T(8,128)(2,1)}, bf16[4,208,512]{2,1,0:T(8,128)(2,1)}, bf16[2,208,512]{2,1,0:T...) custom-call(s32[1]{0:T(128)} %bitcast.refs_0_, ...), custom_call_target="tpu_custom_call" | custom-call | flops 38168166400 | bytes 66519040 | tf_op jit(solution)/shard_map/gather/pallas_call | solution.py:616
  361.5 43.9 %slice_grads.1 = (f32[16,512,128]{2,1,0:T(8,128)}, bf16[16,512,128]{2,1,0:T(8,128)(2,1)}, f32[16,128,512]{2,1,0:T(8,128)}, bf16[16,128,512]{2,1,0:T(8,128)(2,1)}...) custom-call(bf16[16,2,80,512]{3,2,1,0:T(8,128)(2,1)} %get-tuple-element.116.refs_0_.refs_1_, ...), custom_call_target="tpu_custom_call" | custom-call | flops 21474836480 | bytes 67108864 | tf_op jit(solution)/shard_map/slice_grads/pallas_call | solution.py:616
  405.4 0.1 collective-permute-start
  405.5 0.5 collective-permute-start.2
  406.0 0.1 collective-permute-start.1
  406.1 0.4 collective-permute-start.3
  406.5 1.4 bitcast_convert_fusion
  407.9 0.1 slice_bitcast_fusion
  408.0 1.1 slice_reduce_fusion
  409.1 1.3 slice.67
  410.5 0.9 slice.70
  411.3 0.7 copy.45
  412.0 0.0 copy-start.3
  412.0 5.0 %emit.1 = bf16[985,512]{1,0:T(8,128)(2,1)} custom-call(s32[1]{0:T(128)S(6)} %copy.47.refs_0_.refs_2_.count_ref, f32[5,208,512]{2,1,0:T(8,128)} %get-tuple-element.110.refs_8_.middle_ref, bf16[5,208,512]{2,1,0:T(8,128)(2,1)} %get-tuple-element.136.own_ref, bf16[5,208,512]{2,1,0:T(8,128)(2,1)} %get-tuple-element.152.refs_0_), custom_call_target="tpu_custom_call" | custom-call | flops 2000000 | bytes 6000000 | tf_op jit(solution)/shard_map/emit/pallas_call | solution.py:565
  417.1 0.0 collective-permute-done.1
  417.1 0.0 copy-done.3
  417.1 0.6 dynamic-slice_add_fusion.1
  417.7 0.0 collective-permute-done.3
  417.7 1.4 dynamic-slice_add_fusion
  419.1 0.0 collective-permute-done
  419.1 0.0 copy-start
  419.1 5.4 %convert_add_fusion.1 = f32[16,512,128]{2,1,0:T(8,128)} fusion(f32[16,512,128]{2,1,0:T(8,128)} %get-tuple-element.185, bf16[16,512,128]{2,1,0:T(8,128)(2,1)} %collective-permute-done), kind=kLoop, calls=%fused_computation.1 | loop fusion | flops 2097152 | bytes 10485760 | tf_op jit(solution)/shard_map/add | solution.py:1806
  424.5 0.0 collective-permute-done.2
  424.5 0.0 copy-done
  424.5 0.0 copy-start.1
  424.5 2.8 convert_add_fusion
  427.4 0.0 copy-done.1
  427.4 1.3 copy.49
  (2 shorter events, 0.0 us)
Async XLA Ops:
  0.7 13.6 %copy-start.2 = (bf16[256,512]{1,0:T(8,128)(2,1)S(1)}, bf16[256,512]{1,0:T(8,128)(2,1)}, u32[]{:S(2)}) copy-start(bf16[256,512]{1,0:T(8,128)(2,1)} %param.29) | copy-start | bytes 786436
  405.4 13.7 %collective-permute-start = (bf16[16,512,128]{2,1,0:T(8,128)(2,1)}, bf16[16,512,128]{2,1,0:T(8,128)(2,1)}, u32[]{:S(2)}, u32[]{:S(2)}) collective-permute-start(bf16[16,512,128]{2,1,0:T(8,128)(2,1)} %get-tuple-element.186), channel_id=1, source_target_pairs={{0,2},{2,0},{4,6},{6,4},{8,10},{10,8},{12,14},{14,12},{16,18},{18,... | collective-permute-start | bytes 6291464 | tf_op jit(solution)/shard_map/ppermute | solution.py:1799
  405.5 19.0 %collective-permute-start.2 = (bf16[16,128,512]{2,1,0:T(8,128)(2,1)}, bf16[16,128,512]{2,1,0:T(8,128)(2,1)S(1)}, u32[]{:S(2)}, u32[]{:S(2)}) collective-permute-start(bf16[16,128,512]{2,1,0:T(8,128)(2,1)} %get-tuple-element.189), channel_id=1, source_target_pairs={{0,2},{2,0},{4,6},{6,4},{8,10},{10,8},{12,14},{14,12},{16,18},{18,... | collective-permute-start | bytes 6291464 | tf_op jit(solution)/shard_map/ppermute | solution.py:1799
  406.0 11.1 %collective-permute-start.1 = (f32[16,1,256]{2,1,0:T(1,128)}, f32[16,1,256]{2,1,0:T(1,128)S(1)}, u32[]{:S(2)}, u32[]{:S(2)}) collective-permute-start(f32[16,1,256]{2,1,0:T(1,128)} %get-tuple-element.187), channel_id=1, source_target_pairs={{0,2},{2,0},{4,6},{6,4},{8,10},{10,8},{12,14},{14,12},{16,18},{18,... | collective-permute-start | bytes 49160 | tf_op jit(solution)/shard_map/ppermute | solution.py:1799
  406.1 11.6 %collective-permute-start.3 = (f32[16,1,512]{2,1,0:T(1,128)}, f32[16,1,512]{2,1,0:T(1,128)S(1)}, u32[]{:S(2)}, u32[]{:S(2)}) collective-permute-start(f32[16,1,512]{2,1,0:T(1,128)} %get-tuple-element.190), channel_id=1, source_target_pairs={{0,2},{2,0},{4,6},{6,4},{8,10},{10,8},{12,14},{14,12},{16,18},{18,... | collective-permute-start | bytes 98312 | tf_op jit(solution)/shard_map/ppermute | solution.py:1799
  412.0 5.0 %copy-start.3 = (f32[16,1,256]{2,1,0:T(1,128)S(1)}, f32[16,1,256]{2,1,0:T(1,128)}, u32[]{:S(2)}) copy-start(f32[16,1,256]{2,1,0:T(1,128)} %get-tuple-element.187) | copy-start | bytes 49156
  419.1 5.4 %copy-start = (f32[16,128,512]{2,1,0:T(8,128)S(1)}, f32[16,128,512]{2,1,0:T(8,128)}, u32[]{:S(2)}) copy-start(f32[16,128,512]{2,1,0:T(8,128)} %get-tuple-element.188) | copy-start | bytes 12582916
  424.5 2.8 copy-start.1

commit v2 on v1

--- a/solution.py
+++ b/solution.py
@@ -341,9 +341,7 @@
     grads = stacked(parts[senders[0] :])
     first = in_ref[0]
     second = out_ref[0]
-    raised = jnp.dot(rows, first, preferred_element_type=jnp.float32) + in_bias_ref[0].astype(
-        jnp.float32
-    )
+    raised = jnp.dot(rows, first, preferred_element_type=jnp.float32) + own_line(in_bias_ref)
     active, slope = gelu_pair(raised)
     active = active.astype(jnp.bfloat16)
     back = lax.dot_general(
@@ -375,11 +373,11 @@
 
     return run(
         lambda *refs: slice_grads_body(*refs, senders=(len(rows), len(grads))),
-        (*rows, *grads, first, first_bias.reshape(experts, 1, hidden), second),
+        (*rows, *grads, first, first_bias, second),
         [pl.BlockSpec((1,) + piece.shape[1:], lambda e: (e, 0, 0, 0)) for piece in (*rows, *grads)]
         + [
             pl.BlockSpec((1, width, part), lambda e: (e, 0, chip())),
-            pl.BlockSpec((1, 1, part), lambda e: (e, 0, chip())),
+            pl.BlockSpec((experts, part), lambda e: (0, chip())),
             pl.BlockSpec((1, part, width), lambda e: (e, chip(), 0)),
         ],
         [by_image(width, half)] * 2 + [by_image(half, width)] * 2 + [by_image(1, part), by_image(1, width)],
@@ -905,6 +903,37 @@
     lanes = iota((1, 128), 1)
     tokens_alive = (alive_images * IMG_TOK).astype(F32)
     load_out[0] = jnp.broadcast_to(jnp.where(lanes == 64, tokens_alive, totals), (8, 128))
+
+
+def pack_body(*refs):
+    lines, (qkv_ref, out_ref, router_ref, wide_ref, tall_ref) = refs[:-5], refs[-5:]
+    rows, part = qkv_ref.shape[0], lines[0].shape[0]
+    wide_ref[:rows] = qkv_ref[...]
+    table = jnp.zeros((16, part), F32)
+    for k, ref in enumerate(lines):
+        line = jnp.broadcast_to(ref[...].astype(F32).reshape(1, part), (16, part))
+        table = jnp.where(iota((16, part), 0) == k, line, table)
+    wide_ref[rows:] = jnp.zeros((16, wide_ref.shape[1]), BF16)
+    wide_ref[rows:, :part] = table.astype(BF16)
+    width = out_ref.shape[1]
+    tall_ref[:, :width] = out_ref[...]
+    tall_ref[:, width:] = jnp.zeros((rows, 128), BF16)
+    tall_ref[:, width : width + EXPERTS] = router_ref[...]
+
+
+def pack_weights(lines, w_qkv, w_out, w_router):
+    rows = w_qkv.shape[0]
+    return pl.pallas_call(
+        pack_body,
+        in_specs=[pl.BlockSpec(memory_space=pltpu.VMEM)] * (len(lines) + 3),
+        out_specs=[pl.BlockSpec(memory_space=pltpu.VMEM)] * 2,
+        out_shape=[
+            jax.ShapeDtypeStruct((rows + 16, w_qkv.shape[1]), BF16),
+            jax.ShapeDtypeStruct((rows, w_out.shape[1] + 128), BF16),
+        ],
+        cost_estimate=pl.CostEstimate(flops=1_000_000, bytes_accessed=2_500_000, transcendentals=0),
+        name="pack_weights",
+    )(*lines, w_qkv, w_out, w_router)
 
 
 def weight_traffic(wide, tall):
@@ -1177,23 +1206,29 @@
     )
 
 
+def own_line(ref):
+    table = ref[...].astype(F32)
+    return jnp.sum(jnp.where(iota(table.shape, 0) == pl.program_id(0), table, 0.0), axis=0, keepdims=True)
+
+
 def expert_body(row_own, row_far, grad_own, grad_far, in_ref, in_bias_ref, out_ref, out_bias_ref, made_own, made_far, back_own, back_far):
     cap, width = row_own.shape[2:]
     hidden = in_ref.shape[2]
     rows = jnp.concatenate([row_own[0, 0], row_far[0, 0]], axis=0)
     grads = jnp.concatenate([grad_own[0, 0], grad_far[0, 0]], axis=0)
+    in_bias = own_line(in_bias_ref)
     made = jnp.zeros((2 * cap, width), F32)
     back = jnp.zeros((2 * cap, width), F32)
     chunk = 512
     for at in range(0, hidden, chunk):
         first = in_ref[0, :, at : at + chunk]
         second = out_ref[0, at : at + chunk, :]
-        raised = dot(rows, first) + in_bias_ref[0, :, at : at + chunk].astype(F32)
+        raised = dot(rows, first) + in_bias[:, at : at + chunk]
         active, slope = gelu_pair(raised)
         made += dot(active.astype(BF16), second)
         draised = (dot_cols(grads, second) * slope).astype(BF16)
         back += dot_cols(draised, first)
-    made = (made + out_bias_ref[0].astype(F32)).astype(BF16)
+    made = (made + own_line(out_bias_ref)).astype(BF16)
     back = back.astype(BF16)
     made_own[0], made_far[0] = made[:cap], made[cap:]
     back_own[0], back_far[0] = back[:cap], back[cap:]
@@ -1212,11 +1247,11 @@
             pair[1],
             pair[1],
             first,
-            first_bias.reshape(experts, 1, hidden),
+            first_bias,
             second,
-            second_bias.reshape(experts, 1, width),
+            second_bias,
         ),
-        rows + rows + [by_image(width, hidden), by_image(1, hidden), by_image(hidden, width), by_image(1, width)],
+        rows + rows + [by_image(width, hidden), resident(first_bias.shape), by_image(hidden, width), resident(second_bias.shape)],
         [out] * 4,
         [jax.ShapeDtypeStruct((experts, cap, width), BF16)] * 4,
         grid=(experts,),
@@ -1718,10 +1753,9 @@
     device = lax.axis_index("rep")
     mine = lax.axis_index("fsdp")
     core = device % 2
-    small = jnp.stack([norm1_gain, norm1_bias, bias_q, bias_v, bias_out, norm2_gain, norm2_bias])
-    small = jnp.pad(small, ((0, 9), (0, 3 * width - small.shape[1])))
-    wide = jnp.concatenate([w_qkv, small], axis=0)
-    tall = jnp.concatenate([w_out, jnp.pad(w_router, ((0, 0), (0, 128 - EXPERTS)))], axis=1)
+    wide, tall = pack_weights(
+        (norm1_gain, norm1_bias, bias_q, bias_v, bias_out, norm2_gain, norm2_bias), w_qkv, w_out, w_router
+    )
     (tok, cot, route, ids, load), (wide_far, tall_far), _ = prepare(
         tokens, cotangent, routes, image_count, capacity, wide, tall, 0
     )

time: 430 us -> 422 us (0.981)
  local copies, waits for them, and re-layouts: 16.8 us -> 9.84 us
    another operation x8 -> x0, local copies, waits for them, and re-layouts: 4.63 us -> none  [by_slice(): jnp.stack([norm1_gain, norm1_bias, bias_q, bias_v, bias_out, norm2_gain,...]
where the time goes in v2:
time: 422 us; the launch traced here: 421 us
  Pallas kernels  393 us (93%)
  other arithmetic  14.2 us (3%)
  local copies, waits for them, and re-layouts  9.84 us (2%)
    pallas_call x9, Pallas kernels, run(): pl.pallas_call(carried, grid=grid, in_specs=list(in_specs) + [anywhere] *...  386 us
  transfers between devices with their start and end apart: 4, of which 0 were waited for; matrix products, arithmetic and copies ran while one was open for 3% of the time, Pallas kernels for 1%

profile of v2, /device:TPU:0, one launch (start us, length us, event | category | flops | bytes accessed | tf_op | source)
XLA Modules:
  0.0 421.1 jit_solution(681584316079616557)
XLA Ops:
  1.9 1.7 copy.40.refs_4_
  3.6 1.4 copy.39.refs_9_
  5.1 2.4 pack_weights.1
  7.5 21.7 %prepare.1 = (bf16[5,208,512]{2,1,0:T(8,128)(2,1)}, bf16[5,208,512]{2,1,0:T(8,128)(2,1)}, s32[5,208,2]{2,1,0:T(8,128)}, f32[5,8,208]{2,1,0:T(8,128)}, f32[1,8,12...) custom-call(s32[1]{0:T(128)S(6)} %copy.44.refs_0_.refs_2_.count_ref, s32[1]{0:T(128)S(6)} %copy.45.refs_1_, ...), custom_call_target="tpu_custom_call" | custom-call | flops 300000000 | bytes 6000000 | tf_op jit(solution)/shard_map/prepare/pallas_call | solution.py:614
  29.2 30.8 %front.1 = (bf16[5,208,1536]{2,1,0:T(8,128)(2,1)}, bf16[5,8,208,208]{3,2,1,0:T(8,128)(2,1)}, bf16[5,208,512]{2,1,0:T(8,128)(2,1)}, f32[5,208,512]{2,1,0:T(8,128)...) custom-call(s32[1]{0:T(128)S(6)} %copy.44.refs_0_.refs_2_.count_ref,, ...), custom_call_target="tpu_custom_call" | custom-call | flops 6000000000 | bytes 16000000 | tf_op jit(solution)/shard_map/front/pallas_call | solution.py:614
  60.0 47.5 %gather.2 = (bf16[16,2,80,512]{3,2,1,0:T(8,128)(2,1)}, bf16[16,2,80,512]{3,2,1,0:T(8,128)(2,1)}, bf16[3,208,512]{2,1,0:T(8,128)(2,1)}, bf16[1,208,512]{2,1,0:T(8...) custom-call(s32[1]{0:T(128)} %bitcast.refs_0_, ...), custom_call_target="tpu_custom_call" | custom-call | flops 5452595200 | bytes 9502720 | tf_op jit(solution)/shard_map/gather/pallas_call | solution.py:614
  107.5 61.3 %expert_layer.1 = (bf16[16,80,512]{2,1,0:T(8,128)(2,1)}, bf16[16,80,512]{2,1,0:T(8,128)(2,1)}, bf16[16,80,512]{2,1,0:T(8,128)(2,1)}, bf16[16,80,512]{2,1,0:T(8,1...) custom-call(bf16[16,2,80,512]{3,2,1,0:T(8,128)(2,1)} %get-tuple-elem, ...), custom_call_target="tpu_custom_call" | custom-call | flops 21474836480 | bytes 67108864 | tf_op jit(solution)/shard_map/expert_layer/pallas_call | solution.py:614
  168.8 0.7 slice_bitcast_fusion.1
  169.5 0.6 slice.51
  170.7 0.7 multiply_divide_fusion
  171.4 1.8 fusion
  173.2 12.4 %combine.2 = (bf16[5,208,512]{2,1,0:T(8,128)(2,1)}, bf16[5,208,512]{2,1,0:T(8,128)(2,1)}, f32[5,8,208]{2,1,0:T(8,128)}, bf16[1,208,512]{2,1,0:T(8,128)(2,1)}, bf...) custom-call(s32[1]{0:T(128)} %bitcast.refs_0_, bf16[16,80,512]{2,1,0:T(8,128)(2,1)} %get-tuple-element.132.refs_1_, ...), custom_call_target="tpu_custom_call" | custom-call | flops 4089446400 | bytes 6000000 | tf_op jit(solution)/shard_map/combine/pallas_call | solution.py:614
  185.7 21.9 %combine.3 = (bf16[5,208,512]{2,1,0:T(8,128)(2,1)}, bf16[5,208,512]{2,1,0:T(8,128)(2,1)}, f32[5,8,208]{2,1,0:T(8,128)}, bf16[1,208,512]{2,1,0:T(8,128)(2,1)}, bf...) custom-call(s32[1]{0:T(128)} %bitcast.refs_0_, ...), custom_call_target="tpu_custom_call" | custom-call | flops 4089446400 | bytes 6000000 | tf_op jit(solution)/shard_map/combine/pallas_call | solution.py:614
  207.6 42.8 %finish.1 = (f32[985,512]{1,0:T(8,128)}, bf16[2,2,2,64,2176]{4,3,2,1,0:T(8,128)(2,1)}, bf16[1,208,512]{2,1,0:T(8,128)(2,1)}, bf16[3,208,512]{2,1,0:T(8,128)(2,1)...) custom-call(bf16[4,208,512]{2,1,0:T(8,128)(2,1)} %get-tuple-element., ...), custom_call_target="tpu_custom_call" | custom-call | flops 12000000000 | bytes 24000000 | tf_op jit(solution)/shard_map/finish/pallas_call | solution.py:614
  250.4 103.7 %gather.3 = (bf16[16,14,80,512]{3,2,1,0:T(8,128)(2,1)}, bf16[16,14,80,512]{3,2,1,0:T(8,128)(2,1)}, bf16[4,208,512]{2,1,0:T(8,128)(2,1)}, bf16[2,208,512]{2,1,0:T...) custom-call(s32[1]{0:T(128)} %bitcast.refs_0_, ...), custom_call_target="tpu_custom_call" | custom-call | flops 38168166400 | bytes 66519040 | tf_op jit(solution)/shard_map/gather/pallas_call | solution.py:614
  354.1 43.8 %slice_grads.1 = (f32[16,512,128]{2,1,0:T(8,128)}, bf16[16,512,128]{2,1,0:T(8,128)(2,1)}, f32[16,128,512]{2,1,0:T(8,128)}, bf16[16,128,512]{2,1,0:T(8,128)(2,1)}...) custom-call(bf16[16,2,80,512]{3,2,1,0:T(8,128)(2,1)} %get-tuple-element.120.refs_0_.refs_1_, ...), custom_call_target="tpu_custom_call" | custom-call | flops 21474836480 | bytes 67108864 | tf_op jit(solution)/shard_map/slice_grads/pallas_call | solution.py:614
  397.9 0.1 collective-permute-start
  397.9 0.5 collective-permute-start.2
  398.4 0.1 collective-permute-start.1
  398.5 0.4 collective-permute-start.3
  399.0 1.4 bitcast_convert_fusion
  400.3 0.1 slice_bitcast_fusion
  400.4 1.1 slice_reduce_fusion
  401.6 1.3 slice.67
  402.9 0.9 slice.70
  403.8 0.7 copy.42
  404.5 0.0 copy-start.2
  404.5 5.0 %emit.1 = bf16[985,512]{1,0:T(8,128)(2,1)} custom-call(s32[1]{0:T(128)S(6)} %copy.44.refs_0_.refs_2_.count_ref, f32[5,208,512]{2,1,0:T(8,128)} %get-tuple-element.114.refs_8_.middle_ref, bf16[5,208,512]{2,1,0:T(8,128)(2,1)} %get-tuple-element.140.own_ref, bf16[5,208,512]{2,1,0:T(8,128)(2,1)} %get-tuple-element.156.refs_0_), custom_call_target="tpu_custom_call" | custom-call | flops 2000000 | bytes 6000000 | tf_op jit(solution)/shard_map/emit/pallas_call | solution.py:563
  409.5 0.0 collective-permute-done.1
  409.5 0.0 copy-done.2
  409.5 0.6 dynamic-slice_add_fusion.1
  410.1 0.0 collective-permute-done.3
  410.2 1.4 dynamic-slice_add_fusion
  411.6 0.0 collective-permute-done
  411.6 0.0 copy-start
  411.6 5.4 %convert_add_fusion.1 = f32[16,512,128]{2,1,0:T(8,128)} fusion(f32[16,512,128]{2,1,0:T(8,128)} %get-tuple-element.189, bf16[16,512,128]{2,1,0:T(8,128)(2,1)} %collective-permute-done), kind=kLoop, calls=%fused_computation.1 | loop fusion | flops 2097152 | bytes 10485760 | tf_op jit(solution)/shard_map/add | solution.py:1840
  417.0 0.0 collective-permute-done.2
  417.0 0.0 copy-done
  417.0 0.0 copy-start.1
  417.0 2.8 convert_add_fusion
  419.8 0.0 copy-done.1
  419.8 1.3 copy.46
  (1 shorter events, 0.0 us)
Async XLA Ops:
  397.9 13.7 %collective-permute-start = (bf16[16,512,128]{2,1,0:T(8,128)(2,1)}, bf16[16,512,128]{2,1,0:T(8,128)(2,1)}, u32[]{:S(2)}, u32[]{:S(2)}) collective-permute-start(bf16[16,512,128]{2,1,0:T(8,128)(2,1)} %get-tuple-element.190), channel_id=1, source_target_pairs={{0,2},{2,0},{4,6},{6,4},{8,10},{10,8},{12,14},{14,12},{16,18},{18,... | collective-permute-start | bytes 6291464 | tf_op jit(solution)/shard_map/ppermute | solution.py:1833
  397.9 19.0 %collective-permute-start.2 = (bf16[16,128,512]{2,1,0:T(8,128)(2,1)}, bf16[16,128,512]{2,1,0:T(8,128)(2,1)S(1)}, u32[]{:S(2)}, u32[]{:S(2)}) collective-permute-start(bf16[16,128,512]{2,1,0:T(8,128)(2,1)} %get-tuple-element.193), channel_id=1, source_target_pairs={{0,2},{2,0},{4,6},{6,4},{8,10},{10,8},{12,14},{14,12},{16,18},{18,... | collective-permute-start | bytes 6291464 | tf_op jit(solution)/shard_map/ppermute | solution.py:1833
  398.4 11.1 %collective-permute-start.1 = (f32[16,1,256]{2,1,0:T(1,128)}, f32[16,1,256]{2,1,0:T(1,128)S(1)}, u32[]{:S(2)}, u32[]{:S(2)}) collective-permute-start(f32[16,1,256]{2,1,0:T(1,128)} %get-tuple-element.191), channel_id=1, source_target_pairs={{0,2},{2,0},{4,6},{6,4},{8,10},{10,8},{12,14},{14,12},{16,18},{18,... | collective-permute-start | bytes 49160 | tf_op jit(solution)/shard_map/ppermute | solution.py:1833
  398.5 11.6 %collective-permute-start.3 = (f32[16,1,512]{2,1,0:T(1,128)}, f32[16,1,512]{2,1,0:T(1,128)S(1)}, u32[]{:S(2)}, u32[]{:S(2)}) collective-permute-start(f32[16,1,512]{2,1,0:T(1,128)} %get-tuple-element.194), channel_id=1, source_target_pairs={{0,2},{2,0},{4,6},{6,4},{8,10},{10,8},{12,14},{14,12},{16,18},{18,... | collective-permute-start | bytes 98312 | tf_op jit(solution)/shard_map/ppermute | solution.py:1833
  404.5 5.0 %copy-start.2 = (f32[16,1,256]{2,1,0:T(1,128)S(1)}, f32[16,1,256]{2,1,0:T(1,128)}, u32[]{:S(2)}) copy-start(f32[16,1,256]{2,1,0:T(1,128)} %get-tuple-element.191) | copy-start | bytes 49156
  411.6 5.4 %copy-start = (f32[16,128,512]{2,1,0:T(8,128)S(1)}, f32[16,128,512]{2,1,0:T(8,128)}, u32[]{:S(2)}) copy-start(f32[16,128,512]{2,1,0:T(8,128)} %get-tuple-element.192) | copy-start | bytes 12582916
  417.0 2.8 copy-start.1

commit v3 on v2

--- a/solution.py
+++ b/solution.py
@@ -1355,7 +1355,7 @@
 def finish_body(
     count_ref, tok_ref, cot_ref, packed_ref, prob_ref, mixed_ref, middle_ref, second_ref, soft_ref, route_ref,
     row_own, row_far, gate_own, gate_far, aux_ref,
-    wide_own, wide_far, tall_own, tall_far, dtok_ref, pack_ref,
+    wide_own, wide_far, tall_own, tall_far, dtok_ref, pack_ref, loss_ref,
     dpacked, wide_ref, tall_ref, dqkv_ref, dout_ref, drouter_ref, dvec_ref,
 ):
     image = pl.program_id(0)
@@ -1384,7 +1384,14 @@
     gate_grads = jnp.transpose(gate_own[0] + gate_far)
     push = (gate_grads[:, 0:1] - gate_grads[:, 1:2]) * soft[:, EXPERTS + 4 : EXPERTS + 5] * soft[:, EXPERTS + 5 : EXPERTS + 6]
     soft = jnp.where(lane < EXPERTS, soft, 0.0)
-    aux = aux_ref[...] * alive
+    loads = aux_ref[0]
+    lanes = iota(loads.shape, 1)
+    live = jnp.sum(jnp.where(lanes == 2 * EXPERTS, loads, 0.0), axis=1, keepdims=True)
+    share = (loads + pltpu.roll(loads, 128 - EXPERTS, 1)) / (2.0 * live)
+    push_all = jnp.where(lanes < EXPERTS, EXPERTS * share / live, 0.0)
+    loss = jnp.sum(push_all * aux_ref[1], axis=1, keepdims=True)
+    loss_ref[...] = jnp.broadcast_to(loss, loads.shape)
+    aux = push_all[0:1] * alive
     dlogits = soft * (aux - jnp.sum(soft * aux, axis=-1, keepdims=True))
     dlogits += jnp.where(lane == route[:, 0:1], push, 0.0) - jnp.where(lane == route[:, 1:2], push, 0.0)
     dlogits = dlogits.astype(BF16)
@@ -1505,14 +1512,14 @@
             by_image(PAD, 2),
             tile,
             by_image(8, PAD),
-            resident((1, 128)),
+            resident((2, 8, 128)),
             resident(wide[0].shape),
             resident(wide[0].shape),
             resident(tall[0].shape),
             resident(tall[0].shape),
         ],
-        [resident((total, width)), resident(pack)],
-        [shape((total, width), F32), shape(pack, BF16)],
+        [resident((total, width)), resident(pack), resident((8, 128))],
+        [shape((total, width), F32), shape(pack, BF16), shape((8, 128), F32)],
         grid=(images,),
         scratch=[
             pltpu.VMEM((PAD, 3 * width), BF16),
@@ -1802,13 +1809,9 @@
     sum_own, drow_own, dgate_own = staged(
         combine, base, *sender(own), made_own, back_own, rounds=evenly(OWN_ROOM, 5, 0.4)
     )
-    loads, prob_total = sums[0, 0:1], sums[1, 0:1]
-    live = loads[:, 64:65]
-    share = (loads[:, :EXPERTS] + loads[:, EXPERTS : 2 * EXPERTS]) / (2.0 * live)
-    aux = jnp.pad(EXPERTS * share / live, ((0, 0), (0, 128 - EXPERTS)))
-    grad_tokens, pack = staged(
+    grad_tokens, pack, loss = staged(
         finish, image_count, tok, cot, (packed, prob, mixed, middle, second, soft), route, drow_own,
-        lambda plan: net.find(plan, "D", far), dgate_own, net.block("G", far), aux, wide, tall, total,
+        lambda plan: net.find(plan, "D", far), dgate_own, net.block("G", far), sums, wide, tall, total,
         rounds=evenly(FINISH_ROOM, 5, 1.5),
     )
     blocks = [block for block in COT_PATHS if block != far]
@@ -1843,7 +1846,7 @@
         lax.dynamic_slice_in_dim(out_bias, device * piece, piece, axis=1),
     )
 
-    balance_loss = jnp.sum(aux * prob_total)
+    balance_loss = loss[0, 0]
     lines = jnp.transpose(owned[:, 4 * width + EXPERTS : 4 * width + EXPERTS + 8])
     owned = (
         lines[0],

time: 422 us -> 419 us (level)
  no operation moved by 1% of the time
where the time goes in v3:
time: 419 us; the launch traced here: 418 us
  Pallas kernels  394 us (94%)
  other arithmetic  11.7 us (3%)
  local copies, waits for them, and re-layouts  9.76 us (2%)
    pallas_call x9, Pallas kernels, run(): pl.pallas_call(carried, grid=grid, in_specs=list(in_specs) + [anywhere] *...  386 us
  transfers between devices with their start and end apart: 4, of which 0 were waited for; matrix products, arithmetic and copies ran while one was open for 3% of the time, Pallas kernels for 1%

profile of v3, /device:TPU:0, one launch (start us, length us, event | category | flops | bytes accessed | tf_op | source)
XLA Modules:
  0.0 418.2 jit_solution(14375308251228582712)
XLA Ops:
  1.9 1.7 copy.40.refs_4_
  3.6 1.4 copy.39.refs_9_
  5.1 2.4 pack_weights.1
  7.5 21.7 %prepare.1 = (bf16[5,208,512]{2,1,0:T(8,128)(2,1)}, bf16[5,208,512]{2,1,0:T(8,128)(2,1)}, s32[5,208,2]{2,1,0:T(8,128)}, f32[5,8,208]{2,1,0:T(8,128)}, f32[1,8,12...) custom-call(s32[1]{0:T(128)S(6)} %copy.44.refs_0_.refs_2_.count_ref, s32[1]{0:T(128)S(6)} %copy.45.refs_1_, ...), custom_call_target="tpu_custom_call" | custom-call | flops 300000000 | bytes 6000000 | tf_op jit(solution)/shard_map/prepare/pallas_call | solution.py:614
  29.2 30.8 %front.1 = (bf16[5,208,1536]{2,1,0:T(8,128)(2,1)}, bf16[5,8,208,208]{3,2,1,0:T(8,128)(2,1)}, bf16[5,208,512]{2,1,0:T(8,128)(2,1)}, f32[5,208,512]{2,1,0:T(8,128)...) custom-call(s32[1]{0:T(128)S(6)} %copy.44.refs_0_.refs_2_.count_ref,, ...), custom_call_target="tpu_custom_call" | custom-call | flops 6000000000 | bytes 16000000 | tf_op jit(solution)/shard_map/front/pallas_call | solution.py:614
  60.0 47.5 %gather.2 = (bf16[16,2,80,512]{3,2,1,0:T(8,128)(2,1)}, bf16[16,2,80,512]{3,2,1,0:T(8,128)(2,1)}, bf16[3,208,512]{2,1,0:T(8,128)(2,1)}, bf16[1,208,512]{2,1,0:T(8...) custom-call(s32[1]{0:T(128)} %bitcast.refs_0_, ...), custom_call_target="tpu_custom_call" | custom-call | flops 5452595200 | bytes 9502720 | tf_op jit(solution)/shard_map/gather/pallas_call | solution.py:614
  107.5 61.4 %expert_layer.1 = (bf16[16,80,512]{2,1,0:T(8,128)(2,1)}, bf16[16,80,512]{2,1,0:T(8,128)(2,1)}, bf16[16,80,512]{2,1,0:T(8,128)(2,1)}, bf16[16,80,512]{2,1,0:T(8,1...) custom-call(bf16[16,2,80,512]{3,2,1,0:T(8,128)(2,1)} %get-tuple-elem, ...), custom_call_target="tpu_custom_call" | custom-call | flops 21474836480 | bytes 67108864 | tf_op jit(solution)/shard_map/expert_layer/pallas_call | solution.py:614
  168.8 12.7 %combine.2 = (bf16[5,208,512]{2,1,0:T(8,128)(2,1)}, bf16[5,208,512]{2,1,0:T(8,128)(2,1)}, f32[5,8,208]{2,1,0:T(8,128)}, bf16[1,208,512]{2,1,0:T(8,128)(2,1)}, bf...) custom-call(s32[1]{0:T(128)} %bitcast.refs_0_, bf16[16,80,512]{2,1,0:T(8,128)(2,1)} %get-tuple-element.133.refs_1_, ...), custom_call_target="tpu_custom_call" | custom-call | flops 4089446400 | bytes 6000000 | tf_op jit(solution)/shard_map/combine/pallas_call | solution.py:614
  181.5 21.9 %combine.3 = (bf16[5,208,512]{2,1,0:T(8,128)(2,1)}, bf16[5,208,512]{2,1,0:T(8,128)(2,1)}, f32[5,8,208]{2,1,0:T(8,128)}, bf16[1,208,512]{2,1,0:T(8,128)(2,1)}, bf...) custom-call(s32[1]{0:T(128)} %bitcast.refs_0_, ...), custom_call_target="tpu_custom_call" | custom-call | flops 4089446400 | bytes 6000000 | tf_op jit(solution)/shard_map/combine/pallas_call | solution.py:614
  203.4 42.9 %finish.1 = (f32[985,512]{1,0:T(8,128)}, bf16[2,2,2,64,2176]{4,3,2,1,0:T(8,128)(2,1)}, f32[8,128]{1,0:T(8,128)}, bf16[1,208,512]{2,1,0:T(8,128)(2,1)}, bf16[3,20...) custom-call(bf16[4,208,512]{2,1,0:T(8,128)(2,1)} %get-tuple-element., ...), custom_call_target="tpu_custom_call" | custom-call | flops 12000000000 | bytes 24000000 | tf_op jit(solution)/shard_map/finish/pallas_call | solution.py:614
  246.3 103.7 %gather.3 = (bf16[16,14,80,512]{3,2,1,0:T(8,128)(2,1)}, bf16[16,14,80,512]{3,2,1,0:T(8,128)(2,1)}, bf16[4,208,512]{2,1,0:T(8,128)(2,1)}, bf16[2,208,512]{2,1,0:T...) custom-call(s32[1]{0:T(128)} %bitcast.refs_0_, ...), custom_call_target="tpu_custom_call" | custom-call | flops 38168166400 | bytes 66519040 | tf_op jit(solution)/shard_map/gather/pallas_call | solution.py:614
  350.0 43.7 %slice_grads.1 = (f32[16,512,128]{2,1,0:T(8,128)}, bf16[16,512,128]{2,1,0:T(8,128)(2,1)}, f32[16,128,512]{2,1,0:T(8,128)}, bf16[16,128,512]{2,1,0:T(8,128)(2,1)}...) custom-call(bf16[16,2,80,512]{3,2,1,0:T(8,128)(2,1)} %get-tuple-element.121.refs_0_.refs_1_, ...), custom_call_target="tpu_custom_call" | custom-call | flops 21474836480 | bytes 67108864 | tf_op jit(solution)/shard_map/slice_grads/pallas_call | solution.py:614
  393.8 0.1 collective-permute-start
  393.8 0.5 collective-permute-start.2
  394.3 0.1 collective-permute-start.1
  394.4 0.4 collective-permute-start.3
  394.8 1.4 bitcast_convert_fusion
  396.2 0.1 slice_bitcast_fusion
  396.3 1.1 slice_reduce_fusion
  397.5 1.3 slice.51
  398.8 0.9 slice.54
  399.7 1.2 slice.36
  400.9 0.7 copy.42
  401.6 0.0 copy-start.2
  401.6 5.0 %emit.1 = bf16[985,512]{1,0:T(8,128)(2,1)} custom-call(s32[1]{0:T(128)S(6)} %copy.44.refs_0_.refs_2_.count_ref, f32[5,208,512]{2,1,0:T(8,128)} %get-tuple-element.115.refs_8_.middle_ref, bf16[5,208,512]{2,1,0:T(8,128)(2,1)} %get-tuple-element.141.own_ref, bf16[5,208,512]{2,1,0:T(8,128)(2,1)} %get-tuple-element.157.refs_0_), custom_call_target="tpu_custom_call" | custom-call | flops 2000000 | bytes 6000000 | tf_op jit(solution)/shard_map/emit/pallas_call | solution.py:563
  406.6 0.0 collective-permute-done.1
  406.6 0.0 copy-done.2
  406.6 0.6 dynamic-slice_add_fusion.1
  407.2 0.0 collective-permute-done.3
  407.2 1.4 dynamic-slice_add_fusion
  408.6 0.0 collective-permute-done
  408.6 0.0 copy-start
  408.6 5.4 %convert_add_fusion.1 = f32[16,512,128]{2,1,0:T(8,128)} fusion(f32[16,512,128]{2,1,0:T(8,128)} %get-tuple-element.191, bf16[16,512,128]{2,1,0:T(8,128)(2,1)} %collective-permute-done), kind=kLoop, calls=%fused_computation.1 | loop fusion | flops 2097152 | bytes 10485760 | tf_op jit(solution)/shard_map/add | solution.py:1843
  414.1 0.0 collective-permute-done.2
  414.1 0.0 copy-done
  414.1 0.0 copy-start.1
  414.1 2.8 convert_add_fusion
  416.9 0.0 copy-done.1
  416.9 1.3 copy.46
  (1 shorter events, 0.0 us)
Async XLA Ops:
  393.8 14.9 %collective-permute-start = (bf16[16,512,128]{2,1,0:T(8,128)(2,1)}, bf16[16,512,128]{2,1,0:T(8,128)(2,1)}, u32[]{:S(2)}, u32[]{:S(2)}) collective-permute-start(bf16[16,512,128]{2,1,0:T(8,128)(2,1)} %get-tuple-element.192), channel_id=1, source_target_pairs={{0,2},{2,0},{4,6},{6,4},{8,10},{10,8},{12,14},{14,12},{16,18},{18,... | collective-permute-start | bytes 6291464 | tf_op jit(solution)/shard_map/ppermute | solution.py:1836
  393.8 20.2 %collective-permute-start.2 = (bf16[16,128,512]{2,1,0:T(8,128)(2,1)}, bf16[16,128,512]{2,1,0:T(8,128)(2,1)S(1)}, u32[]{:S(2)}, u32[]{:S(2)}) collective-permute-start(bf16[16,128,512]{2,1,0:T(8,128)(2,1)} %get-tuple-element.195), channel_id=1, source_target_pairs={{0,2},{2,0},{4,6},{6,4},{8,10},{10,8},{12,14},{14,12},{16,18},{18,... | collective-permute-start | bytes 6291464 | tf_op jit(solution)/shard_map/ppermute | solution.py:1836
  394.3 12.3 %collective-permute-start.1 = (f32[16,1,256]{2,1,0:T(1,128)}, f32[16,1,256]{2,1,0:T(1,128)S(1)}, u32[]{:S(2)}, u32[]{:S(2)}) collective-permute-start(f32[16,1,256]{2,1,0:T(1,128)} %get-tuple-element.193), channel_id=1, source_target_pairs={{0,2},{2,0},{4,6},{6,4},{8,10},{10,8},{12,14},{14,12},{16,18},{18,... | collective-permute-start | bytes 49160 | tf_op jit(solution)/shard_map/ppermute | solution.py:1836
  394.4 12.8 %collective-permute-start.3 = (f32[16,1,512]{2,1,0:T(1,128)}, f32[16,1,512]{2,1,0:T(1,128)S(1)}, u32[]{:S(2)}, u32[]{:S(2)}) collective-permute-start(f32[16,1,512]{2,1,0:T(1,128)} %get-tuple-element.196), channel_id=1, source_target_pairs={{0,2},{2,0},{4,6},{6,4},{8,10},{10,8},{12,14},{14,12},{16,18},{18,... | collective-permute-start | bytes 98312 | tf_op jit(solution)/shard_map/ppermute | solution.py:1836
  401.6 5.0 %copy-start.2 = (f32[16,1,256]{2,1,0:T(1,128)S(1)}, f32[16,1,256]{2,1,0:T(1,128)}, u32[]{:S(2)}) copy-start(f32[16,1,256]{2,1,0:T(1,128)} %get-tuple-element.193) | copy-start | bytes 49156
  408.6 5.4 %copy-start = (f32[16,128,512]{2,1,0:T(8,128)S(1)}, f32[16,128,512]{2,1,0:T(8,128)}, u32[]{:S(2)}) copy-start(f32[16,128,512]{2,1,0:T(8,128)} %get-tuple-element.194) | copy-start | bytes 12582916
  414.1 2.8 copy-start.1

commit v4 on v3

--- a/solution.py
+++ b/solution.py
@@ -844,15 +844,15 @@
     return centred * scale, scale
 
 
-def prep_body(count_ref, cap_ref, tok_ref, cot_ref, route_ref, tok_out, cot_out, route_out, ids_out, load_out, wide, narrow):
+def prep_body(count_ref, cap_ref, tok_ref, cot_ref, route_ref, tok_out, cot_out, route_out, ids_out, load_out, wide, narrow, lines):
     pl.when(pl.program_id(0) == 0)(
         lambda: prep_rows(
-            count_ref, cap_ref, tok_ref, cot_ref, route_ref, tok_out, cot_out, route_out, ids_out, load_out, wide, narrow
+            count_ref, cap_ref, tok_ref, cot_ref, route_ref, tok_out, cot_out, route_out, ids_out, load_out, wide, narrow, lines
         )
     )
 
 
-def prep_rows(count_ref, cap_ref, tok_ref, cot_ref, route_ref, tok_out, cot_out, route_out, ids_out, load_out, wide, narrow):
+def prep_rows(count_ref, cap_ref, tok_ref, cot_ref, route_ref, tok_out, cot_out, route_out, ids_out, load_out, wide, narrow, lines):
     images = tok_out.shape[0]
     total = tok_ref.shape[0]
     alive_images = count_ref[0]
@@ -867,7 +867,9 @@
     for image in range(images):
         tok_out[image] = jnp.where(real, split(wide, image), 0.0).astype(BF16)
     wide[pl.ds(0, total), :] = cot_ref[...].astype(F32)
-    narrow[pl.ds(0, total), :] = route_ref[...]
+    lines[...] = jnp.zeros_like(lines)
+    lines[0:2, 0:total] = route_ref[...].astype(F32)
+    narrow[...] = jnp.transpose(lines[...])[: narrow.shape[0], :2].astype(jnp.int32)
     routes = []
     lives = []
     for image in range(images):
@@ -971,7 +973,7 @@
         [resident(a.shape) for a in shapes],
         shapes,
         grid=(2,),
-        scratch=[pltpu.VMEM((1000, width), F32), pltpu.VMEM((1000, 2), jnp.int32)],
+        scratch=[pltpu.VMEM((1000, width), F32), pltpu.VMEM((1000, 2), jnp.int32), pltpu.VMEM((8, 1024), F32)],
         cost=pl.CostEstimate(flops=300_000_000, bytes_accessed=6_000_000, transcendentals=0),
         name="prepare",
         traffic=weight_traffic(wide, tall),
@@ -1764,7 +1766,7 @@
         (norm1_gain, norm1_bias, bias_q, bias_v, bias_out, norm2_gain, norm2_bias), w_qkv, w_out, w_router
     )
     (tok, cot, route, ids, load), (wide_far, tall_far), _ = prepare(
-        tokens, cotangent, routes, image_count, capacity, wide, tall, 0
+        tokens, cotangent, routes.T, image_count, capacity, wide, tall, 0
     )
     wide, tall = (wide, wide_far), (tall, tall_far)
     base = (mine * (local * CAP)).reshape(1)

time: 419 us -> 417 us (level)
  no operation moved by 1% of the time
where the time goes in v4:
time: 417 us; the launch traced here: 416 us
  Pallas kernels  393 us (94%)
  other arithmetic  11.7 us (3%)
  local copies, waits for them, and re-layouts  8.06 us (2%)
    pallas_call x9, Pallas kernels, run(): pl.pallas_call(carried, grid=grid, in_specs=list(in_specs) + [anywhere] *...  386 us
  transfers between devices with their start and end apart: 4, of which 0 were waited for; matrix products, arithmetic and copies ran while one was open for 3% of the time, Pallas kernels for 1%

profile of v4, /device:TPU:0, one launch (start us, length us, event | category | flops | bytes accessed | tf_op | source)
XLA Modules:
  0.0 416.4 jit_solution(3728627168388187854)
XLA Ops:
  1.9 1.5 copy.38.refs_9_
  3.4 2.4 pack_weights.1
  5.8 21.6 %prepare.1 = (bf16[5,208,512]{2,1,0:T(8,128)(2,1)}, bf16[5,208,512]{2,1,0:T(8,128)(2,1)}, s32[5,208,2]{2,1,0:T(8,128)}, f32[5,8,208]{2,1,0:T(8,128)}, f32[1,8,12...) custom-call(s32[1]{0:T(128)S(6)} %copy.42.refs_0_.refs_2_.count_ref, s32[1]{0:T(128)S(6)} %copy.43.refs_1_, ...), custom_call_target="tpu_custom_call" | custom-call | flops 300000000 | bytes 6000000 | tf_op jit(solution)/shard_map/prepare/pallas_call | solution.py:614
  27.3 30.8 %front.1 = (bf16[5,208,1536]{2,1,0:T(8,128)(2,1)}, bf16[5,8,208,208]{3,2,1,0:T(8,128)(2,1)}, bf16[5,208,512]{2,1,0:T(8,128)(2,1)}, f32[5,208,512]{2,1,0:T(8,128)...) custom-call(s32[1]{0:T(128)S(6)} %copy.42.refs_0_.refs_2_.count_ref,, ...), custom_call_target="tpu_custom_call" | custom-call | flops 6000000000 | bytes 16000000 | tf_op jit(solution)/shard_map/front/pallas_call | solution.py:614
  58.2 47.5 %gather.2 = (bf16[16,2,80,512]{3,2,1,0:T(8,128)(2,1)}, bf16[16,2,80,512]{3,2,1,0:T(8,128)(2,1)}, bf16[3,208,512]{2,1,0:T(8,128)(2,1)}, bf16[1,208,512]{2,1,0:T(8...) custom-call(s32[1]{0:T(128)} %bitcast.1.refs_0_, ...), custom_call_target="tpu_custom_call" | custom-call | flops 5452595200 | bytes 9502720 | tf_op jit(solution)/shard_map/gather/pallas_call | solution.py:614
  105.6 61.4 %expert_layer.1 = (bf16[16,80,512]{2,1,0:T(8,128)(2,1)}, bf16[16,80,512]{2,1,0:T(8,128)(2,1)}, bf16[16,80,512]{2,1,0:T(8,128)(2,1)}, bf16[16,80,512]{2,1,0:T(8,1...) custom-call(bf16[16,2,80,512]{3,2,1,0:T(8,128)(2,1)} %get-tuple-elem, ...), custom_call_target="tpu_custom_call" | custom-call | flops 21474836480 | bytes 67108864 | tf_op jit(solution)/shard_map/expert_layer/pallas_call | solution.py:614
  167.0 12.7 %combine.2 = (bf16[5,208,512]{2,1,0:T(8,128)(2,1)}, bf16[5,208,512]{2,1,0:T(8,128)(2,1)}, f32[5,8,208]{2,1,0:T(8,128)}, bf16[1,208,512]{2,1,0:T(8,128)(2,1)}, bf...) custom-call(s32[1]{0:T(128)} %bitcast.1.refs_0_, bf16[16,80,512]{2,1,0:T(8,128)(2,1)} %get-tuple-element.133.refs_1_, ...), custom_call_target="tpu_custom_call" | custom-call | flops 4089446400 | bytes 6000000 | tf_op jit(solution)/shard_map/combine/pallas_call | solution.py:614
  179.7 21.9 %combine.3 = (bf16[5,208,512]{2,1,0:T(8,128)(2,1)}, bf16[5,208,512]{2,1,0:T(8,128)(2,1)}, f32[5,8,208]{2,1,0:T(8,128)}, bf16[1,208,512]{2,1,0:T(8,128)(2,1)}, bf...) custom-call(s32[1]{0:T(128)} %bitcast.1.refs_0_, ...), custom_call_target="tpu_custom_call" | custom-call | flops 4089446400 | bytes 6000000 | tf_op jit(solution)/shard_map/combine/pallas_call | solution.py:614
  201.5 42.9 %finish.1 = (f32[985,512]{1,0:T(8,128)}, bf16[2,2,2,64,2176]{4,3,2,1,0:T(8,128)(2,1)}, f32[8,128]{1,0:T(8,128)}, bf16[1,208,512]{2,1,0:T(8,128)(2,1)}, bf16[3,20...) custom-call(bf16[4,208,512]{2,1,0:T(8,128)(2,1)} %get-tuple-element., ...), custom_call_target="tpu_custom_call" | custom-call | flops 12000000000 | bytes 24000000 | tf_op jit(solution)/shard_map/finish/pallas_call | solution.py:614
  244.4 103.7 %gather.3 = (bf16[16,14,80,512]{3,2,1,0:T(8,128)(2,1)}, bf16[16,14,80,512]{3,2,1,0:T(8,128)(2,1)}, bf16[4,208,512]{2,1,0:T(8,128)(2,1)}, bf16[2,208,512]{2,1,0:T...) custom-call(s32[1]{0:T(128)} %bitcast.1.refs_0_, ...), custom_call_target="tpu_custom_call" | custom-call | flops 38168166400 | bytes 66519040 | tf_op jit(solution)/shard_map/gather/pallas_call | solution.py:614
  348.2 43.8 %slice_grads.1 = (f32[16,512,128]{2,1,0:T(8,128)}, bf16[16,512,128]{2,1,0:T(8,128)(2,1)}, f32[16,128,512]{2,1,0:T(8,128)}, bf16[16,128,512]{2,1,0:T(8,128)(2,1)}...) custom-call(bf16[16,2,80,512]{3,2,1,0:T(8,128)(2,1)} %get-tuple-element.121.refs_0_.refs_1_, ...), custom_call_target="tpu_custom_call" | custom-call | flops 21474836480 | bytes 67108864 | tf_op jit(solution)/shard_map/slice_grads/pallas_call | solution.py:614
  391.9 0.1 collective-permute-start
  392.0 0.5 collective-permute-start.2
  392.5 0.1 collective-permute-start.1
  392.6 0.4 collective-permute-start.3
  393.0 1.4 bitcast_convert_fusion
  394.4 0.1 slice_bitcast_fusion
  394.5 1.1 slice_reduce_fusion
  395.6 1.3 slice.51
  397.0 0.9 slice.54
  397.9 1.2 slice.36
  399.0 0.7 copy.40
  399.7 0.0 copy-start.2
  399.7 5.0 %emit.1 = bf16[985,512]{1,0:T(8,128)(2,1)} custom-call(s32[1]{0:T(128)S(6)} %copy.42.refs_0_.refs_2_.count_ref, f32[5,208,512]{2,1,0:T(8,128)} %get-tuple-element.115.refs_8_.middle_ref, bf16[5,208,512]{2,1,0:T(8,128)(2,1)} %get-tuple-element.141.own_ref, bf16[5,208,512]{2,1,0:T(8,128)(2,1)} %get-tuple-element.157.refs_0_), custom_call_target="tpu_custom_call" | custom-call | flops 2000000 | bytes 6000000 | tf_op jit(solution)/shard_map/emit/pallas_call | solution.py:563
  404.8 0.0 collective-permute-done.1
  404.8 0.0 copy-done.2
  404.8 0.6 dynamic-slice_add_fusion.1
  405.4 0.0 collective-permute-done.3
  405.4 1.4 dynamic-slice_add_fusion
  406.8 0.0 collective-permute-done
  406.8 0.0 copy-start
  406.8 5.4 %convert_add_fusion.1 = f32[16,512,128]{2,1,0:T(8,128)} fusion(f32[16,512,128]{2,1,0:T(8,128)} %get-tuple-element.191, bf16[16,512,128]{2,1,0:T(8,128)(2,1)} %collective-permute-done), kind=kLoop, calls=%fused_computation.1 | loop fusion | flops 2097152 | bytes 10485760 | tf_op jit(solution)/shard_map/add | solution.py:1845
  412.2 0.0 collective-permute-done.2
  412.2 0.0 copy-done
  412.2 0.0 copy-start.1
  412.2 2.8 convert_add_fusion
  415.1 0.0 copy-done.1
  415.1 1.3 copy.44
  (1 shorter events, 0.0 us)
Async XLA Ops:
  391.9 14.9 %collective-permute-start = (bf16[16,512,128]{2,1,0:T(8,128)(2,1)}, bf16[16,512,128]{2,1,0:T(8,128)(2,1)}, u32[]{:S(2)}, u32[]{:S(2)}) collective-permute-start(bf16[16,512,128]{2,1,0:T(8,128)(2,1)} %get-tuple-element.192), channel_id=1, source_target_pairs={{0,2},{2,0},{4,6},{6,4},{8,10},{10,8},{12,14},{14,12},{16,18},{18,... | collective-permute-start | bytes 6291464 | tf_op jit(solution)/shard_map/ppermute | solution.py:1838
  392.0 20.2 %collective-permute-start.2 = (bf16[16,128,512]{2,1,0:T(8,128)(2,1)}, bf16[16,128,512]{2,1,0:T(8,128)(2,1)S(1)}, u32[]{:S(2)}, u32[]{:S(2)}) collective-permute-start(bf16[16,128,512]{2,1,0:T(8,128)(2,1)} %get-tuple-element.195), channel_id=1, source_target_pairs={{0,2},{2,0},{4,6},{6,4},{8,10},{10,8},{12,14},{14,12},{16,18},{18,... | collective-permute-start | bytes 6291464 | tf_op jit(solution)/shard_map/ppermute | solution.py:1838
  392.5 12.3 %collective-permute-start.1 = (f32[16,1,256]{2,1,0:T(1,128)}, f32[16,1,256]{2,1,0:T(1,128)S(1)}, u32[]{:S(2)}, u32[]{:S(2)}) collective-permute-start(f32[16,1,256]{2,1,0:T(1,128)} %get-tuple-element.193), channel_id=1, source_target_pairs={{0,2},{2,0},{4,6},{6,4},{8,10},{10,8},{12,14},{14,12},{16,18},{18,... | collective-permute-start | bytes 49160 | tf_op jit(solution)/shard_map/ppermute | solution.py:1838
  392.6 12.8 %collective-permute-start.3 = (f32[16,1,512]{2,1,0:T(1,128)}, f32[16,1,512]{2,1,0:T(1,128)S(1)}, u32[]{:S(2)}, u32[]{:S(2)}) collective-permute-start(f32[16,1,512]{2,1,0:T(1,128)} %get-tuple-element.196), channel_id=1, source_target_pairs={{0,2},{2,0},{4,6},{6,4},{8,10},{10,8},{12,14},{14,12},{16,18},{18,... | collective-permute-start | bytes 98312 | tf_op jit(solution)/shard_map/ppermute | solution.py:1838
  399.7 5.0 %copy-start.2 = (f32[16,1,256]{2,1,0:T(1,128)S(1)}, f32[16,1,256]{2,1,0:T(1,128)}, u32[]{:S(2)}) copy-start(f32[16,1,256]{2,1,0:T(1,128)} %get-tuple-element.193) | copy-start | bytes 49156
  406.8 5.4 %copy-start = (f32[16,128,512]{2,1,0:T(8,128)S(1)}, f32[16,128,512]{2,1,0:T(8,128)}, u32[]{:S(2)}) copy-start(f32[16,128,512]{2,1,0:T(8,128)} %get-tuple-element.194) | copy-start | bytes 12582916
  412.2 2.8 copy-start.1
